TPU v7x, 32 devices: a whole 2x2x4 slice. The times are simulated.
32 devices in a mesh: ens: 2 (over x), lon: 4 (over y, core), lat: 4 (over z).
Axes of the slice: x: 2, y: 2, z: 4, core: 2. Of those that a mesh axis runs over, the one named last changes fastest.
Arguments:
- fields: bfloat16 [8, 768, 1024], P(('ens', 'lat'), 'lon'), parts along dimension 0, may hold values from -6 to 6
- conv_weight: bfloat16 [9216, 1024], P(None, 'lon'), may hold values from -0.0625 to 0.0625
- norm_gain: float32 [1024], replicated, may hold values from 0.1 to 1.9
- qkv_weight: bfloat16 [1024, 3072], replicated, may hold values from -0.1875 to 0.1875
- out_weight: bfloat16 [1024, 1024], replicated, may hold values from -0.1875 to 0.1875
- key_bias: bfloat16 [4, 768, 16], P('lat', 'lon'), may hold values from -8 to 250
Outputs:
- mixed: bfloat16 [8, 768, 1024], P(('ens', 'lat'), 'lon'), parts along dimension 0
There are 2 independent parts, one for each index of `ens`. A program takes and returns all parts, laid end to end along the dimension named above; an argument that names none is the same for every part. Nothing has to cross between parts.
All inputs are finite; a program needn't handle non-finite values.
Results may differ from a plain program's by a relative error of at most 0.012.
Values may be sent and summed in bfloat16 or wider, within the bound.
No kernel may reach another device: no remote copies, remote signals or barrier semaphores. Data moves between devices by JAX's collectives and lax.ppermute only.
A program may use at most 128 MiB of HBM per device.

v0:
```python
import math

import jax
import jax.numpy as jnp
from jax import lax
from jax.experimental import pallas as pl
from jax.experimental.pallas import tpu as pltpu
from jax.sharding import PartitionSpec as P


H = 16
EDGE = 16
PIECES = 8
F32 = jnp.float32
BF16 = jnp.bfloat16


def extended(block, sides, width):
    for axis, dim in sides:
        count = lax.axis_size(axis)
        forward = [(i, i + 1) for i in range(count - 1)]
        backward = [(target, source) for source, target in forward]
        low = lax.ppermute(
            lax.slice_in_dim(block, block.shape[dim] - width, None, axis=dim), axis, forward
        )
        high = lax.ppermute(lax.slice_in_dim(block, 0, width, axis=dim), axis, backward)
        block = jnp.concatenate([low, block, high], axis=dim)
    return block


def tap_sum(wrapped, conv_weight, out_rows, lon_total, channels):
    out_width = conv_weight.shape[1]
    accum_cols = jnp.zeros((out_rows * lon_total, out_width), jnp.float32)
    tap_idx = 0
    for step_lat in (-1, 0, 1):
        for step_lon in (-1, 0, 1):
            shifted = wrapped[
                1 + step_lat : 1 + step_lat + out_rows, 1 + step_lon : 1 + step_lon + lon_total
            ].reshape(out_rows * lon_total, channels)
            accum_cols = accum_cols + jnp.dot(
                shifted,
                conv_weight[tap_idx * channels : (tap_idx + 1) * channels],
                preferred_element_type=jnp.float32,
            )
            tap_idx += 1
    return accum_cols.reshape(out_rows, lon_total, out_width)


def general_device(fields, conv_weight, norm_gain, qkv_weight, out_weight, key_bias):
    lat_n, lon_n, channels = fields.shape
    row_count = lat_n * lon_n
    head_dim = channels // H
    score_scale = 1.0 / math.sqrt(head_dim)
    banded = extended(fields, (("lat", 0),), 1)
    circle = lax.all_gather(banded, "lon", axis=1, tiled=True)
    lon_total = circle.shape[1]
    wrapped = jnp.concatenate([circle[:, -1:], circle, circle[:, :1]], axis=1)
    out_cols = tap_sum(wrapped, conv_weight, lat_n, lon_total, channels).astype(jnp.bfloat16)
    conv_out = lax.all_to_all(out_cols, "lon", split_axis=1, concat_axis=2, tiled=True).reshape(
        row_count, channels
    )
    residual = (
        fields.reshape(row_count, channels).astype(jnp.float32) + conv_out.astype(jnp.float32)
    ).astype(jnp.bfloat16)
    stream = residual.astype(jnp.float32)
    normed = (
        stream * lax.rsqrt(jnp.mean(stream * stream, axis=-1, keepdims=True) + 1e-06) * norm_gain
    ).astype(jnp.bfloat16)
    projected = jnp.dot(normed, qkv_weight, preferred_element_type=jnp.float32).astype(jnp.bfloat16)
    queries = projected[:, :channels].reshape(lat_n, lon_n, channels)
    key_rows = projected[:, channels : 2 * channels].reshape(lat_n, lon_n, channels)
    value_rows = projected[:, 2 * channels :].reshape(lat_n, lon_n, channels)
    query_heads = queries.reshape(lat_n, lon_n, H, head_dim)
    key_part = lax.all_gather(key_rows, "lon", axis=1, tiled=True)
    value_part = lax.all_gather(value_rows, "lon", axis=1, tiled=True)
    bias_part = lax.all_gather(key_bias, "lon", axis=1, tiled=True)
    span = key_part.shape[1]
    key_heads = key_part.reshape(lat_n, span, H, head_dim)
    value_heads = value_part.reshape(lat_n, span, H, head_dim)
    scores = (
        jnp.einsum("aqhd,akhd->ahqk", query_heads, key_heads, preferred_element_type=jnp.float32)
        * score_scale
    )
    scores = scores + jnp.transpose(bias_part, (0, 2, 1)).astype(jnp.float32)[:, :, None, :]
    weights = jnp.exp(scores - jnp.max(scores, axis=-1)[..., None])
    denom = jnp.sum(weights, axis=-1)
    accum = jnp.einsum(
        "ahqk,akhd->ahqd",
        weights.astype(jnp.bfloat16),
        value_heads,
        preferred_element_type=jnp.float32,
    )
    attended = (
        jnp.transpose(accum / denom[..., None], (0, 2, 1, 3))
        .reshape(row_count, channels)
        .astype(jnp.bfloat16)
    )
    mixed = residual.astype(jnp.float32) + jnp.dot(
        attended, out_weight, preferred_element_type=jnp.float32
    )
    return mixed.astype(jnp.bfloat16).reshape(lat_n, lon_n, channels)


VMEM = pltpu.VMEM
ANY = pl.ANY


def vspec():
    return pl.BlockSpec(memory_space=VMEM)


def sspec():
    return pl.BlockSpec(memory_space=pltpu.SMEM)


def aspec():
    return pl.BlockSpec(memory_space=ANY)


def vout(shape, dtype):
    return VMEM(shape, dtype)


def load_kernel(*refs):
    count = (len(refs) - 1) // 2
    sem = refs[-1]
    copies = []
    for src, dst in zip(refs[:count], refs[count : 2 * count]):
        rows = src.shape[0]
        pieces = PIECES if rows % (16 * PIECES) == 0 else 1
        size = rows // pieces
        for p in range(pieces):
            at = pl.ds(p * size, size)
            copy = pltpu.make_async_copy(src.at[at], dst.at[at], sem.at[len(copies)])
            copy.start()
            copies.append(copy)
    for copy in copies:
        copy.wait()


def load(*arrays):
    total = sum(a.size * a.dtype.itemsize for a in arrays)
    return pl.pallas_call(
        load_kernel,
        out_shape=tuple(vout(a.shape, a.dtype) for a in arrays),
        in_specs=[aspec()] * len(arrays),
        out_specs=tuple(vspec() for _ in arrays),
        scratch_shapes=[pltpu.SemaphoreType.DMA((PIECES * len(arrays),))],
        compiler_params=pltpu.CompilerParams(vmem_limit_bytes=1 << 20),
        cost_estimate=pl.CostEstimate(flops=0, bytes_accessed=total, transcendentals=0),
        name="load",
    )(*[pltpu.with_memory_space_constraint(a, pltpu.HBM) for a in arrays])


def conv_kernel(me, xa, xb, ea, eb, w, first, second, mid, ext, cols):
    n, ch = xa.shape
    core = me[0] % 2
    if ea.shape[0] == EDGE:
        edge_a, edge_b = ea[...], eb[...]
    else:
        edge_a = ea[pl.ds(pl.multiple_of(core * (n - EDGE), 16), EDGE), :]
        edge_b = eb[pl.ds(pl.multiple_of((1 - core) * (n - EDGE), 16), EDGE), :]
    odd = me[1] % 2
    ext[pl.ds(pl.multiple_of(EDGE + core * n, 16), n), :] = xa[...]
    ext[pl.ds(pl.multiple_of(EDGE + (1 - core) * n, 16), n), :] = xb[...]
    far = EDGE + 2 * n
    ext[pl.ds(pl.multiple_of((1 - core) * far, 16), EDGE), :] = edge_a
    ext[pl.ds(pl.multiple_of(core * far, 16), EDGE), :] = edge_b
    for b in range(3):
        cols[:, b * ch : (b + 1) * ch] = ext[EDGE - 1 + b : EDGE - 1 + b + 2 * n, :]
    for a, out in ((2 * odd, first), (2 - 2 * odd, second), (1, mid)):
        taps = w[pl.ds(pl.multiple_of(a * 3 * ch, 16), 3 * ch), :]
        out[...] = jnp.dot(cols[...], taps, preferred_element_type=F32).astype(out.dtype)


def conv_half(me, xa, xb, ea, eb, w):
    n, ch = xa.shape
    width = w.shape[1]
    return pl.pallas_call(
        conv_kernel,
        out_shape=(
            vout((2 * n, width), BF16),
            vout((2 * n, width), BF16),
            vout((2 * n, width), F32),
        ),
        in_specs=[sspec()] + [vspec()] * 5,
        out_specs=(vspec(),) * 3,
        scratch_shapes=[
            VMEM((2 * n + 2 * EDGE, ch), BF16),
            VMEM((2 * n, 3 * ch), BF16),
        ],
        compiler_params=pltpu.CompilerParams(vmem_limit_bytes=12 << 20),
        cost_estimate=pl.CostEstimate(
            flops=2 * 2 * n * 9 * ch * width, bytes_accessed=2 * 9 * ch * width, transcendentals=0
        ),
        name="conv_half",
    )(me, xa, xb, ea, eb, w)


def residual_kernel(me, first, second, mid, xa, xb, *rest):
    out = rest[-1]
    n = xa.shape[0]
    width = mid.shape[1]
    lane = me[0]
    core = lane % 2
    at = pl.ds(pl.multiple_of(lane * width, width), width)
    for x, place in ((xa, core), (xb, 1 - core)):
        rows = pl.ds(pl.multiple_of(place * n, 16), n)
        conv_out = first[rows, :].astype(F32) + second[rows, :].astype(F32) + mid[rows, :]
        out[rows, :] = (x[:, at].astype(F32) + conv_out.astype(BF16).astype(F32)).astype(BF16)
    if len(rest) == 2:
        out[2 * n : 2 * n + H, :] = rest[0][...]


def residual_of(me, first, second, mid, xa, xb, *extra):
    rows, width = mid.shape
    rows += H * len(extra)
    return pl.pallas_call(
        residual_kernel,
        out_shape=vout((rows, width), BF16),
        in_specs=[sspec()] + [vspec()] * (5 + len(extra)),
        out_specs=vspec(),
        compiler_params=pltpu.CompilerParams(vmem_limit_bytes=4 << 20),
        cost_estimate=pl.CostEstimate(
            flops=4 * rows * width, bytes_accessed=8 * rows * width, transcendentals=0
        ),
        name="residual_of",
    )(me, first, second, mid, xa, xb, *extra)


def normed_of(blocks, gain, lane, ch, rows):
    streams = [b[0:rows, :].astype(F32) for b in blocks]
    square = sum(jnp.sum(s * s, axis=-1, keepdims=True) for s in streams)
    factor = lax.rsqrt(square * (1.0 / ch) + 1e-06)
    return [(s * factor * gain[lane ^ k]).astype(BF16) for k, s in enumerate(streams)]


def keys_kernel(me, b0, b1, b2, b3, gain, w, k_out, v_out):
    lane = me[0]
    rows, ch = k_out.shape
    width = b0.shape[1]
    parts = normed_of((b0, b1, b2, b3), gain, lane, ch, rows)
    for out, first in ((k_out, ch), (v_out, 2 * ch)):
        acc = None
        for k, part in enumerate(parts):
            at = pl.multiple_of((lane ^ k) * width, width)
            term = jnp.dot(part, w[pl.ds(at, width), first : first + ch], preferred_element_type=F32)
            acc = term if acc is None else acc + term
        out[...] = acc.astype(BF16)


def keys_of(me, blocks, gain, w):
    rows = blocks[0].shape[0]
    ch = w.shape[0]
    out = vout((rows, ch), BF16)
    return pl.pallas_call(
        keys_kernel,
        out_shape=(out, out),
        in_specs=[sspec()] + [vspec()] * 6,
        out_specs=(vspec(), vspec()),
        compiler_params=pltpu.CompilerParams(vmem_limit_bytes=24 << 20),
        cost_estimate=pl.CostEstimate(
            flops=2 * rows * ch * 2 * ch, bytes_accessed=4 * ch * ch, transcendentals=0
        ),
        name="keys_of",
    )(me, *blocks, gain, w)


def attend_kernel(
    me, b0, b1, b2, b3, gain, w, k_far, v_far, bias_y, bias_d, w_out, out, keys, values, query, attended
):
    lane = me[0]
    core = lane % 2
    n, ch = out.shape
    rows = 2 * n
    width = b0.shape[1]
    hd = ch // H
    blocks = (b0, b1, b2, b3)
    parts = normed_of(blocks, gain, lane, ch, rows)
    for first, dst in ((ch, keys), (2 * ch, values), (0, query)):
        acc = None
        for k, part in enumerate(parts):
            at = pl.multiple_of((lane ^ k) * width, width)
            term = jnp.dot(part, w[pl.ds(at, width), first : first + ch], preferred_element_type=F32)
            acc = term if acc is None else acc + term
        dst[0:rows, :] = acc.astype(BF16)
    keys[rows : 2 * rows, :] = k_far[...]
    values[rows : 2 * rows, :] = v_far[...]
    pieces = []
    for a, c in ((b0, b1), (bias_y, bias_d)):
        a, c = (v[rows : rows + H, 0:n].astype(F32) for v in (a, c))
        pieces += [jnp.where(core == 0, a, c), jnp.where(core == 0, c, a)]
    bias = jnp.concatenate(pieces, axis=1)
    own = pl.multiple_of(core * n, 16)
    group = 256 // hd
    head_of = lax.broadcasted_iota(jnp.int32, (n, 256), 1) // hd
    for g in range(ch // 256):
        cols = slice(g * 256, (g + 1) * 256)
        q = query[pl.ds(own, n), cols] * jnp.asarray(1.0 / math.sqrt(hd), BF16)
        stacked = jnp.concatenate(
            [jnp.where(head_of == t, q, jnp.zeros_like(q)) for t in range(group)], axis=0
        )
        scores = lax.dot_general(
            stacked, keys[:, cols], (((1,), (1,)), ((), ())), preferred_element_type=F32
        )
        values_g = values[:, cols]
        result = jnp.zeros((n, 256), F32)
        for t in range(group):
            head = g * group + t
            s = scores[t * n : (t + 1) * n] + bias[head : head + 1, :]
            e = jnp.exp(s - jnp.max(s, axis=-1, keepdims=True))
            total = jnp.sum(e, axis=-1, keepdims=True)
            o = jnp.dot(e.astype(BF16), values_g, preferred_element_type=F32)
            result = jnp.where(head_of == t, o / total, result)
        attended[:, cols] = result.astype(BF16)
    for k, block in enumerate(blocks):
        at = pl.multiple_of((lane ^ k) * width, width)
        mixed = block[pl.ds(own, n), :].astype(F32) + jnp.dot(
            attended[...], w_out[:, pl.ds(at, width)], preferred_element_type=F32
        )
        out[:, pl.ds(at, width)] = mixed.astype(BF16)


def attend(me, blocks, gain, w, k_far, v_far, bias_y, bias_d, w_out):
    rows, ch = k_far.shape
    n = rows // 2
    return pl.pallas_call(
        attend_kernel,
        out_shape=jax.ShapeDtypeStruct((n, ch), BF16),
        in_specs=[sspec()] + [vspec()] * 11,
        out_specs=vspec(),
        scratch_shapes=[
            VMEM((2 * rows, ch), BF16),
            VMEM((2 * rows, ch), BF16),
            VMEM((rows, ch), BF16),
            VMEM((n, ch), BF16),
        ],
        compiler_params=pltpu.CompilerParams(vmem_limit_bytes=40 << 20),
        cost_estimate=pl.CostEstimate(
            flops=2 * rows * ch * 3 * ch + 4 * n * 2 * rows * ch * 4,
            bytes_accessed=8 * ch * ch,
            transcendentals=n * 2 * rows * H,
        ),
        name="attend",
    )(me, *blocks, gain, w, k_far, v_far, bias_y, bias_d, w_out)


def four_shard_device(fields, conv_weight, norm_gain, qkv_weight, out_weight, key_bias):
    _, n, ch = fields.shape
    width = conv_weight.shape[1]
    lane = lax.axis_index("lon")
    core = lane % 2
    me = jnp.stack([lane, lax.axis_index("lat")]).astype(jnp.int32)
    lon_size = lax.axis_size("lon")
    lat_size = lax.axis_size("lat")

    def swap(value, bit):
        return lax.ppermute(value, "lon", [(i, i ^ bit) for i in range(lon_size)])

    def lat_swap(value, first):
        pairs = [(i, i + 1) for i in range(first, lat_size - 1, 2)]
        return lax.ppermute(value, "lat", pairs + [(b, a) for a, b in pairs])

    x = fields.reshape(n, ch)
    edge = lax.dynamic_slice_in_dim(x, core * (n - EDGE), EDGE, axis=0)
    edge_y = swap(edge, 2)
    x_c = swap(x, 1)
    x_y = swap(x, 2)
    edge_d = swap(edge_y, 1)
    x_d = swap(x_y, 1)
    bias_own = jnp.pad(key_bias.reshape(n, H).T, ((0, 0), (0, width - n)))
    x_v, conv_w = load(x, conv_weight)
    near_parts = conv_half(me, x_v, x_c, edge_y, edge_d, conv_w)
    za = lat_swap(near_parts[0], 0)
    zb = lat_swap(near_parts[1], 1)
    near = residual_of(me, za, zb, near_parts[2], x_v, x_c, bias_own)
    far_y = swap(near, 2)
    near_c = swap(near, 1)
    far_d = swap(far_y, 1)
    far_parts = conv_half(me, x_y, x_d, x_v, x_c, conv_w)
    za = lat_swap(far_parts[0], 0)
    zb = lat_swap(far_parts[1], 1)
    far = residual_of(me, za, zb, far_parts[2], x_y, x_d)
    near_y = swap(far, 2)
    far_c = swap(far, 1)
    near_d = swap(near_y, 1)

    gain = norm_gain.reshape(lon_size, 1, width)
    k_far, v_far = keys_of(me, (far, far_c, far_y, far_d), gain, qkv_weight)
    out = attend(me, (near, near_c, near_y, near_d), gain, qkv_weight, k_far, v_far, far_y, far_d, out_weight)
    return out.reshape(fields.shape)


def solution(mesh):
    def on_device(*args):
        fields, conv_weight = args[0], args[1]
        special = (
            mesh.shape["lon"] == 4
            and fields.shape[0] == 1
            and conv_weight.shape[1] % 256 == 0
            and fields.shape[1] % 32 == 0
            and fields.shape[1] <= conv_weight.shape[1]
        )
        if not special:
            return general_device(*args)
        return four_shard_device(*args)

    return jax.shard_map(
        on_device,
        mesh=mesh,
        in_specs=(
            P(("ens", "lat"), "lon", None),
            P(None, "lon"),
            P(),
            P(),
            P(),
            P("lat", "lon", None),
        ),
        out_specs=P(("ens", "lat"), "lon", None),
        check_vma=False,
    )
```

profile of v0, /device:TPU:0, one launch (start us, length us, event | category | flops | bytes accessed | tf_op | source)
XLA Modules:
  0.0 55.9 jit_solution(9647070217544697530)
XLA Ops:
  0.0 3.0 %collective-permute-start.6 = (bf16[192,1024]{1,0:T(8,128)(2,1)}, bf16[192,1024]{1,0:T(8,128)(2,1)S(1)}, u32[]{:S(2)}, u32[]{:S(2)}) collective-permute-start(bf16[192,1024]{1,0:T(8,128)(2,1)} %bitcast.14), channel_id=1, source_target_pairs={{0,8},{4,12},{8,0},{12,4},{1,9},{5,13},{9,1},{13,5},{2,10},{6,14},... | collective-permute-start | bytes 1179656 | tf_op jit(solution)/shard_map/ppermute | solution.py:358
  3.0 9.3 %collective-permute-done.6.xa = bf16[192,1024]{1,0:T(8,128)(2,1)S(1)} collective-permute-done((bf16[192,1024]{1,0:T(8,128)(2,1)}, bf16[192,1024]{1,0:T(8,128)(2,1)S(1)}, u32[]{:S(2)}, u32[]{:S(2)}) %collective-permute-start.6) | collective-permute-done | bytes 393248 | tf_op jit(solution)/shard_map/ppermute | solution.py:358
  12.3 0.0 collective-permute-start.7
  12.3 0.8 %dynamic-slice_bitcast_fusion = bf16[16,1024]{1,0:T(8,128)(2,1)S(1)} fusion(bf16[1,192,1024]{2,1,0:T(8,128)(2,1)} %param.6, s32[]{:T(128)S(6)} %select_n.11), kind=kLoop, calls=%fused_computation | loop fusion | bytes 65540 | tf_op jit(solution)/shard_map/dynamic_slice | solution.py:365
  13.1 1.7 %collective-permute-start.1 = (bf16[16,1024]{1,0:T(8,128)(2,1)S(1)}, bf16[16,1024]{1,0:T(8,128)(2,1)S(1)}, u32[]{:S(2)}, u32[]{:S(2)}) collective-permute-start(bf16[16,1024]{1,0:T(8,128)(2,1)S(1)} %dynamic-slice_bitcast_fusion), channel_id=1, source_target_pairs={{0,8},{4,12},{8,0},{12,4},{1,9},{5,13},{9,1},{13,5},{2,10},{6,14},... | collective-permute-start | bytes 98312 | tf_op jit(solution)/shard_map/ppermute | solution.py:358
  14.8 2.2 %collective-permute-done.1.ea = bf16[16,1024]{1,0:T(8,128)(2,1)S(1)} collective-permute-done((bf16[16,1024]{1,0:T(8,128)(2,1)S(1)}, bf16[16,1024]{1,0:T(8,128)(2,1)S(1)}, u32[]{:S(2)}, u32[]{:S(2)}) %collective-permute-start.1) | collective-permute-done | bytes 32800 | tf_op jit(solution)/shard_map/ppermute | solution.py:358
  17.0 0.0 collective-permute-start.2
  17.0 0.1 pad_add_fusion.me
  17.1 2.6 %load.1 = (bf16[192,1024]{1,0:T(8,128)(2,1)S(1)}, bf16[9216,256]{1,0:T(8,128)(2,1)S(1)}) custom-call(bf16[192,1024]{1,0:T(8,128)(2,1)} %bitcast.16, bf16[9216,256]{1,0:T(8,128)(2,1)} %refs_1_.1), custom_call_target="tpu_custom_call" | custom-call | bytes 5111808 | tf_op jit(solution)/shard_map/load/pallas_call | solution.py:143
  19.7 0.0 collective-permute-done.xb.eb
  19.7 0.0 slice-start
  19.7 2.7 %conv_half.2 = (bf16[384,256]{1,0:T(8,128)(2,1)S(1)}, bf16[384,256]{1,0:T(8,128)(2,1)S(1)}, f32[384,256]{1,0:T(8,128)S(1)}) custom-call(s32[2]{0:T(128)S(1)} %pad_add_fusion.me, bf16[192,1024]{1,0:T(8,128)(2,1)S(1)} %get-tuple-element.15.xa.ea, bf16[192,1024]{1,0:T(8,128)(2,1)S(1)} %collective-permute-done.xb.eb, ...), custom_call_target="tpu_custom_call" | custom-call | flops 1811939328 | bytes 4718592 | tf_op jit(solution)/shard_map/conv_half/pallas_call | solution.py:179
  22.4 0.0 copy-start.2
  22.4 1.9 %collective-permute-start.3 = (bf16[384,256]{1,0:T(8,128)(2,1)S(1)}, bf16[384,256]{1,0:T(8,128)(2,1)S(1)}, u32[]{:S(2)}, u32[]{:S(2)}) collective-permute-start(bf16[384,256]{1,0:T(8,128)(2,1)S(1)} %get-tuple-element.17), channel_id=1, source_target_pairs={{0,1},{2,3},{1,0},{3,2},{4,5},{6,7},{5,4},{7,6},{8,9},{10,11},{9,8... | collective-permute-start | bytes 589832 | tf_op jit(solution)/shard_map/ppermute | solution.py:362
  24.2 0.8 %collective-permute-start.4 = (bf16[384,256]{1,0:T(8,128)(2,1)S(1)}, bf16[384,256]{1,0:T(8,128)(2,1)S(1)}, u32[]{:S(2)}, u32[]{:S(2)}) collective-permute-start(bf16[384,256]{1,0:T(8,128)(2,1)S(1)} %get-tuple-element.18), channel_id=1, source_target_pairs={{1,2},{2,1},{5,6},{6,5},{9,10},{10,9},{13,14},{14,13},{17,18},{18,... | collective-permute-start | bytes 589832 | tf_op jit(solution)/shard_map/ppermute | solution.py:362
  25.0 0.0 collective-permute-done.7.xb
  25.1 2.7 %conv_half.3 = (bf16[384,256]{1,0:T(8,128)(2,1)S(1)}, bf16[384,256]{1,0:T(8,128)(2,1)S(1)}, f32[384,256]{1,0:T(8,128)S(1)}) custom-call(s32[2]{0:T(128)S(1)} %pad_add_fusion.me, bf16[192,1024]{1,0:T(8,128)(2,1)S(1)} %collective-permute-done.6.xa, bf16[192,1024]{1,0:T(8,128)(2,1)S(1)} %collective-permute-done.7.xb, ...), custom_call_target="tpu_custom_call" | custom-call | flops 1811939328 | bytes 4718592 | tf_op jit(solution)/shard_map/conv_half/pallas_call | solution.py:179
  27.7 4.5 %collective-permute-start.8 = (bf16[384,256]{1,0:T(8,128)(2,1)S(1)}, bf16[384,256]{1,0:T(8,128)(2,1)S(1)}, u32[]{:S(2)}, u32[]{:S(2)}) collective-permute-start(bf16[384,256]{1,0:T(8,128)(2,1)S(1)} %get-tuple-element.20), channel_id=1, source_target_pairs={{0,1},{2,3},{1,0},{3,2},{4,5},{6,7},{5,4},{7,6},{8,9},{10,11},{9,8... | collective-permute-start | bytes 589832 | tf_op jit(solution)/shard_map/ppermute | solution.py:362
  32.2 0.8 %collective-permute-start.9 = (bf16[384,256]{1,0:T(8,128)(2,1)S(1)}, bf16[384,256]{1,0:T(8,128)(2,1)S(1)}, u32[]{:S(2)}, u32[]{:S(2)}) collective-permute-start(bf16[384,256]{1,0:T(8,128)(2,1)S(1)} %get-tuple-element.21), channel_id=1, source_target_pairs={{1,2},{2,1},{5,6},{6,5},{9,10},{10,9},{13,14},{14,13},{17,18},{18,... | collective-permute-start | bytes 589832 | tf_op jit(solution)/shard_map/ppermute | solution.py:362
  33.1 0.0 collective-permute-done.4.second
  33.1 0.7 %residual_of.2.b0 = bf16[400,256]{1,0:T(8,128)(2,1)S(1)} custom-call(s32[2]{0:T(128)S(1)} %pad_add_fusion.me, bf16[384,256]{1,0:T(8,128)(2,1)S(1)} %collective-permute-done.3.first, bf16[384,256]{1,0:T(8,128)(2,1)S(1)} %collective-permute-done.4.second, f32[384,256]{1,0:T(8,128)S(1)} %get-tuple-element.19.mid, ...), custom_call_target="tpu_custom_call" | custom-call | flops 409600 | bytes 819200 | tf_op jit(solution)/shard_map/residual_of/pallas_call | solution.py:218
  33.8 0.0 copy-start.1
  33.8 1.6 %collective-permute-start.13 = (bf16[400,256]{1,0:T(8,128)(2,1)S(1)}, bf16[400,256]{1,0:T(8,128)(2,1)S(1)}, u32[]{:S(2)}, u32[]{:S(2)}) collective-permute-start(bf16[400,256]{1,0:T(8,128)(2,1)S(1)} %residual_of.2.b0), channel_id=1, source_target_pairs={{0,8},{4,12},{8,0},{12,4},{1,9},{5,13},{9,1},{13,5},{2,10},{6,14},... | collective-permute-start | bytes 614408 | tf_op jit(solution)/shard_map/ppermute | solution.py:358
  35.3 1.8 %collective-permute-done.8.first = bf16[384,256]{1,0:T(8,128)(2,1)S(1)} collective-permute-done((bf16[384,256]{1,0:T(8,128)(2,1)S(1)}, bf16[384,256]{1,0:T(8,128)(2,1)S(1)}, u32[]{:S(2)}, u32[]{:S(2)}) %collective-permute-start.8) | collective-permute-done | bytes 196640 | tf_op jit(solution)/shard_map/ppermute | solution.py:362
  37.2 0.7 %residual_of.3.b0 = bf16[384,256]{1,0:T(8,128)(2,1)S(1)} custom-call(s32[2]{0:T(128)S(1)} %pad_add_fusion.me, bf16[384,256]{1,0:T(8,128)(2,1)S(1)} %collective-permute-done.8.first, bf16[384,256]{1,0:T(8,128)(2,1)S(1)} %collective-permute-done.9.second, f32[384,256]{1,0:T(8,128)S(1)} %get-tuple-element.22.mid, ...), custom_call_target="tpu_custom_call" | custom-call | flops 393216 | bytes 786432 | tf_op jit(solution)/shard_map/residual_of/pallas_call | solution.py:218
  37.9 1.6 %collective-permute-start.10 = (bf16[384,256]{1,0:T(8,128)(2,1)S(1)}, bf16[384,256]{1,0:T(8,128)(2,1)S(1)}, u32[]{:S(2)}, u32[]{:S(2)}) collective-permute-start(bf16[384,256]{1,0:T(8,128)(2,1)S(1)} %residual_of.3.b0), channel_id=1, source_target_pairs={{0,8},{4,12},{8,0},{12,4},{1,9},{5,13},{9,1},{13,5},{2,10},{6,14},... | collective-permute-start | bytes 589832 | tf_op jit(solution)/shard_map/ppermute | solution.py:358
  39.5 1.6 %collective-permute-done.13.b2.bias_y = bf16[400,256]{1,0:T(8,128)(2,1)S(1)} collective-permute-done((bf16[400,256]{1,0:T(8,128)(2,1)S(1)}, bf16[400,256]{1,0:T(8,128)(2,1)S(1)}, u32[]{:S(2)}, u32[]{:S(2)}) %collective-permute-start.13) | collective-permute-done | bytes 204832 | tf_op jit(solution)/shard_map/ppermute | solution.py:358
  41.1 0.5 collective-permute-start.12
  41.6 0.0 collective-permute-start.5
  41.6 3.1 %collective-permute-done.10.b2 = bf16[384,256]{1,0:T(8,128)(2,1)S(1)} collective-permute-done((bf16[384,256]{1,0:T(8,128)(2,1)S(1)}, bf16[384,256]{1,0:T(8,128)(2,1)S(1)}, u32[]{:S(2)}, u32[]{:S(2)}) %collective-permute-start.10) | collective-permute-done | bytes 196640 | tf_op jit(solution)/shard_map/ppermute | solution.py:358
  44.7 2.5 %keys_of.1 = (bf16[384,1024]{1,0:T(8,128)(2,1)S(1)}, bf16[384,1024]{1,0:T(8,128)(2,1)S(1)}) custom-call(s32[2]{0:T(128)S(1)} %pad_add_fusion.me, bf16[384,256]{1,0:T(8,128)(2,1)S(1)} %residual_of.3.b0, bf16[384,256]{1,0:T(8,128)(2,1)S(1)} %collective-permute-done.12.b1, bf16[400,256]{1,0:T(8,128)(2,1)S(1)} %collective-permute-done.13.b2.bias_y, ...), custom_call_target="tpu_custom_call" | custom-call | flops 1610612736 | bytes 4194304 | tf_op jit(solution)/shard_map/keys_of/pallas_call | solution.py:256
  47.3 8.6 %attend.1 = bf16[192,1024]{1,0:T(8,128)(2,1)} custom-call(s32[2]{0:T(128)S(1)} %pad_add_fusion.me, bf16[400,256]{1,0:T(8,128)(2,1)S(1)} %residual_of.2.b0, bf16[400,256]{1,0:T(8,128)(2,1)S(1)} %collective-permute-done.5.b1, bf16[384,256]{1,0:T(8,128)(2,1)S(1)} %collective-permute-done.10.b2, bf16[384,256]{1,0:T(8,128)(2,1)S(1)} %collective-permute-done.11.b3, ...), custom_call_target="tpu_custom_call" | custom-call | flops 4831838208 | bytes 8388608 | tf_op jit(solution)/shard_map/attend/pallas_call | solution.py:327
  (19 shorter events, 0.0 us)
Async XLA Ops:
  0.0 12.3 %collective-permute-start.6 = (bf16[192,1024]{1,0:T(8,128)(2,1)}, bf16[192,1024]{1,0:T(8,128)(2,1)S(1)}, u32[]{:S(2)}, u32[]{:S(2)}) collective-permute-start(bf16[192,1024]{1,0:T(8,128)(2,1)} %bitcast.14), channel_id=1, source_target_pairs={{0,8},{4,12},{8,0},{12,4},{1,9},{5,13},{9,1},{13,5},{2,10},{6,14},... | collective-permute-start | bytes 1179656 | tf_op jit(solution)/shard_map/ppermute | solution.py:358
  3.0 16.7 %collective-permute-start = (bf16[192,1024]{1,0:T(8,128)(2,1)}, bf16[192,1024]{1,0:T(8,128)(2,1)S(1)}, u32[]{:S(2)}, u32[]{:S(2)}) collective-permute-start(bf16[192,1024]{1,0:T(8,128)(2,1)} %bitcast.15), channel_id=1, source_target_pairs={{0,4},{4,0},{8,12},{12,8},{1,5},{5,1},{9,13},{13,9},{2,6},{6,2},{1... | collective-permute-start | bytes 1179656 | tf_op jit(solution)/shard_map/ppermute | solution.py:358
  12.3 12.7 %collective-permute-start.7 = (bf16[192,1024]{1,0:T(8,128)(2,1)S(1)}, bf16[192,1024]{1,0:T(8,128)(2,1)S(1)}, u32[]{:S(2)}, u32[]{:S(2)}) collective-permute-start(bf16[192,1024]{1,0:T(8,128)(2,1)S(1)} %collective-permute-done.6.xa), channel_id=1, source_target_pairs={{0,4},{4,0},{8,12},{12,8},{1,5},{5,1},{9,13},{13,9},{2,6},{6,2},{1... | collective-permute-start | bytes 1179656 | tf_op jit(solution)/shard_map/ppermute | solution.py:358
  13.1 3.9 %collective-permute-start.1 = (bf16[16,1024]{1,0:T(8,128)(2,1)S(1)}, bf16[16,1024]{1,0:T(8,128)(2,1)S(1)}, u32[]{:S(2)}, u32[]{:S(2)}) collective-permute-start(bf16[16,1024]{1,0:T(8,128)(2,1)S(1)} %dynamic-slice_bitcast_fusion), channel_id=1, source_target_pairs={{0,8},{4,12},{8,0},{12,4},{1,9},{5,13},{9,1},{13,5},{2,10},{6,14},... | collective-permute-start | bytes 98312 | tf_op jit(solution)/shard_map/ppermute | solution.py:358
  17.0 2.7 %collective-permute-start.2 = (bf16[16,1024]{1,0:T(8,128)(2,1)S(1)}, bf16[16,1024]{1,0:T(8,128)(2,1)S(1)}, u32[]{:S(2)}, u32[]{:S(2)}) collective-permute-start(bf16[16,1024]{1,0:T(8,128)(2,1)S(1)} %collective-permute-done.1.ea), channel_id=1, source_target_pairs={{0,4},{4,0},{8,12},{12,8},{1,5},{5,1},{9,13},{13,9},{2,6},{6,2},{1... | collective-permute-start | bytes 98312 | tf_op jit(solution)/shard_map/ppermute | solution.py:358
  19.7 25.0 %slice-start = ((s8[6291456]{0:T(1024)(128)(4,1)}), s8[4194304]{0:T(1024)(128)(4,1)S(1)}, s32[]{:S(2)}) async-start(s8[6291456]{0:T(1024)(128)(4,1)} %bitcast.10), calls=%async_computation | async-start | bytes 8388608
  22.4 10.7 %copy-start.2 = (bf16[1,192,16]{1,2,0:T(8,128)(2,1)S(1)}, bf16[1,192,16]{1,2,0:T(8,128)(2,1)}, u32[]{:S(2)}) copy-start(bf16[1,192,16]{1,2,0:T(8,128)(2,1)} %param.11) | copy-start | bytes 18436
  22.4 10.7 %collective-permute-start.3 = (bf16[384,256]{1,0:T(8,128)(2,1)S(1)}, bf16[384,256]{1,0:T(8,128)(2,1)S(1)}, u32[]{:S(2)}, u32[]{:S(2)}) collective-permute-start(bf16[384,256]{1,0:T(8,128)(2,1)S(1)} %get-tuple-element.17), channel_id=1, source_target_pairs={{0,1},{2,3},{1,0},{3,2},{4,5},{6,7},{5,4},{7,6},{8,9},{10,11},{9,8... | collective-permute-start | bytes 589832 | tf_op jit(solution)/shard_map/ppermute | solution.py:362
  24.2 20.5 %slice-start.1 = ((s8[6291456]{0:T(1024)(128)(4,1)}), s8[2097152]{0:T(1024)(128)(4,1)S(1)}, s32[]{:S(2)}) async-start(s8[6291456]{0:T(1024)(128)(4,1)} %bitcast.10), calls=%async_computation.1 | async-start | bytes 4194304
  24.2 20.5 %copy-start = (f32[1024]{0:T(1024)S(1)}, f32[1024]{0:T(1024)}, u32[]{:S(2)}) copy-start(f32[1024]{0:T(1024)} %param.8) | copy-start | bytes 12292
  24.2 8.8 %collective-permute-start.4 = (bf16[384,256]{1,0:T(8,128)(2,1)S(1)}, bf16[384,256]{1,0:T(8,128)(2,1)S(1)}, u32[]{:S(2)}, u32[]{:S(2)}) collective-permute-start(bf16[384,256]{1,0:T(8,128)(2,1)S(1)} %get-tuple-element.18), channel_id=1, source_target_pairs={{1,2},{2,1},{5,6},{6,5},{9,10},{10,9},{13,14},{14,13},{17,18},{18,... | collective-permute-start | bytes 589832 | tf_op jit(solution)/shard_map/ppermute | solution.py:362
  27.7 9.5 %collective-permute-start.8 = (bf16[384,256]{1,0:T(8,128)(2,1)S(1)}, bf16[384,256]{1,0:T(8,128)(2,1)S(1)}, u32[]{:S(2)}, u32[]{:S(2)}) collective-permute-start(bf16[384,256]{1,0:T(8,128)(2,1)S(1)} %get-tuple-element.20), channel_id=1, source_target_pairs={{0,1},{2,3},{1,0},{3,2},{4,5},{6,7},{5,4},{7,6},{8,9},{10,11},{9,8... | collective-permute-start | bytes 589832 | tf_op jit(solution)/shard_map/ppermute | solution.py:362
  32.2 5.0 %collective-permute-start.9 = (bf16[384,256]{1,0:T(8,128)(2,1)S(1)}, bf16[384,256]{1,0:T(8,128)(2,1)S(1)}, u32[]{:S(2)}, u32[]{:S(2)}) collective-permute-start(bf16[384,256]{1,0:T(8,128)(2,1)S(1)} %get-tuple-element.21), channel_id=1, source_target_pairs={{1,2},{2,1},{5,6},{6,5},{9,10},{10,9},{13,14},{14,13},{17,18},{18,... | collective-permute-start | bytes 589832 | tf_op jit(solution)/shard_map/ppermute | solution.py:362
  33.8 13.5 %copy-start.1 = (bf16[1024,1024]{1,0:T(8,128)(2,1)S(1)}, bf16[1024,1024]{1,0:T(8,128)(2,1)}, u32[]{:S(2)}) copy-start(bf16[1024,1024]{1,0:T(8,128)(2,1)} %w_out.1) | copy-start | bytes 6291460
  33.8 7.3 %collective-permute-start.13 = (bf16[400,256]{1,0:T(8,128)(2,1)S(1)}, bf16[400,256]{1,0:T(8,128)(2,1)S(1)}, u32[]{:S(2)}, u32[]{:S(2)}) collective-permute-start(bf16[400,256]{1,0:T(8,128)(2,1)S(1)} %residual_of.2.b0), channel_id=1, source_target_pairs={{0,8},{4,12},{8,0},{12,4},{1,9},{5,13},{9,1},{13,5},{2,10},{6,14},... | collective-permute-start | bytes 614408 | tf_op jit(solution)/shard_map/ppermute | solution.py:358
  37.9 6.8 %collective-permute-start.10 = (bf16[384,256]{1,0:T(8,128)(2,1)S(1)}, bf16[384,256]{1,0:T(8,128)(2,1)S(1)}, u32[]{:S(2)}, u32[]{:S(2)}) collective-permute-start(bf16[384,256]{1,0:T(8,128)(2,1)S(1)} %residual_of.3.b0), channel_id=1, source_target_pairs={{0,8},{4,12},{8,0},{12,4},{1,9},{5,13},{9,1},{13,5},{2,10},{6,14},... | collective-permute-start | bytes 589832 | tf_op jit(solution)/shard_map/ppermute | solution.py:358
  41.1 3.6 %collective-permute-start.14 = (bf16[400,256]{1,0:T(8,128)(2,1)S(1)}, bf16[400,256]{1,0:T(8,128)(2,1)S(1)}, u32[]{:S(2)}, u32[]{:S(2)}) collective-permute-start(bf16[400,256]{1,0:T(8,128)(2,1)S(1)} %collective-permute-done.13.b2.bias_y), channel_id=1, source_target_pairs={{0,4},{4,0},{8,12},{12,8},{1,5},{5,1},{9,13},{13,9},{2,6},{6,2},{1... | collective-permute-start | bytes 614408 | tf_op jit(solution)/shard_map/ppermute | solution.py:358
  41.1 3.6 %collective-permute-start.12 = (bf16[384,256]{1,0:T(8,128)(2,1)S(1)}, bf16[384,256]{1,0:T(8,128)(2,1)S(1)}, u32[]{:S(2)}, u32[]{:S(2)}) collective-permute-start(bf16[384,256]{1,0:T(8,128)(2,1)S(1)} %residual_of.3.b0), channel_id=1, source_target_pairs={{0,4},{4,0},{8,12},{12,8},{1,5},{5,1},{9,13},{13,9},{2,6},{6,2},{1... | collective-permute-start | bytes 589832 | tf_op jit(solution)/shard_map/ppermute | solution.py:358
  41.6 5.7 %collective-permute-start.5 = (bf16[400,256]{1,0:T(8,128)(2,1)S(1)}, bf16[400,256]{1,0:T(8,128)(2,1)S(1)}, u32[]{:S(2)}, u32[]{:S(2)}) collective-permute-start(bf16[400,256]{1,0:T(8,128)(2,1)S(1)} %residual_of.2.b0), channel_id=1, source_target_pairs={{0,4},{4,0},{8,12},{12,8},{1,5},{5,1},{9,13},{13,9},{2,6},{6,2},{1... | collective-permute-start | bytes 614408 | tf_op jit(solution)/shard_map/ppermute | solution.py:358
  44.7 2.6 %collective-permute-start.11 = (bf16[384,256]{1,0:T(8,128)(2,1)S(1)}, bf16[384,256]{1,0:T(8,128)(2,1)S(1)}, u32[]{:S(2)}, u32[]{:S(2)}) collective-permute-start(bf16[384,256]{1,0:T(8,128)(2,1)S(1)} %collective-permute-done.10.b2), channel_id=1, source_target_pairs={{0,4},{4,0},{8,12},{12,8},{1,5},{5,1},{9,13},{13,9},{2,6},{6,2},{1... | collective-permute-start | bytes 589832 | tf_op jit(solution)/shard_map/ppermute | solution.py:358
where the time goes:
time: 56.5 us; the launch traced here: 55.9 us
  Pallas kernels  20.3 us (36%)
  waiting for transfers between devices  18.1 us (32%)
  starting transfers between devices  16.4 us (29%)
  local copies, waits for them, and re-layouts  0.8 us (1%)
    ppermute x11, waiting for transfers between devices, swap(): return lax.ppermute(value, 'lon', [(i, i ^ bit) for i in range(lon_size)])  16.2 us
    pallas_call x1, Pallas kernels, attend(): pl.pallas_call(attend_kernel, out_shape=jax.ShapeDtypeStruct((n, ch), BF1...  8.58 us
    ppermute x11, starting transfers between devices, swap(): return lax.ppermute(value, 'lon', [(i, i ^ bit) for i in range(lon_size)])  8.43 us
    ppermute x4, starting transfers between devices, lat_swap(): return lax.ppermute(value, 'lat', pairs + [(b, a) for a, b in pairs])  7.95 us
    pallas_call x2, Pallas kernels, conv_half(): pl.pallas_call(conv_kernel, out_shape=(vout((2 * n, width), BF16), vout((...  5.33 us
    pallas_call x1, Pallas kernels, load(): pl.pallas_call(load_kernel, out_shape=tuple((vout(a.shape, a.dtype) for a...  2.57 us
    pallas_call x1, Pallas kernels, keys_of(): pl.pallas_call(keys_kernel, out_shape=(out, out), in_specs=[sspec()] + [v...  2.51 us
    ppermute x4, waiting for transfers between devices, lat_swap(): return lax.ppermute(value, 'lat', pairs + [(b, a) for a, b in pairs])  1.86 us
  transfers between devices with their start and end apart: 15, of which 5 were waited for; matrix products, arithmetic and copies ran while one was open for 2% of the time, Pallas kernels for 21%

commit v1 on v0

--- a/solution.py
+++ b/solution.py
@@ -1,3 +1,4 @@
+import functools
 import math
 
 import jax
@@ -203,10 +204,13 @@
     width = mid.shape[1]
     lane = me[0]
     core = lane % 2
+    inner = jnp.logical_and(me[1] > 0, me[1] < me[2] - 1)
     at = pl.ds(pl.multiple_of(lane * width, width), width)
     for x, place in ((xa, core), (xb, 1 - core)):
         rows = pl.ds(pl.multiple_of(place * n, 16), n)
-        conv_out = first[rows, :].astype(F32) + second[rows, :].astype(F32) + mid[rows, :]
+        south = second[rows, :].astype(F32)
+        south = jnp.where(inner, south, jnp.zeros_like(south))
+        conv_out = first[rows, :].astype(F32) + south + mid[rows, :]
         out[rows, :] = (x[:, at].astype(F32) + conv_out.astype(BF16).astype(F32)).astype(BF16)
     if len(rest) == 2:
         out[2 * n : 2 * n + H, :] = rest[0][...]
@@ -266,8 +270,57 @@
     )(me, *blocks, gain, w)
 
 
+def scaled(block, gain, lane, k, rows):
+    return (block[0:rows, :].astype(F32) * gain[lane ^ k]).astype(BF16)
+
+
+def project_kernel(steps, me, gain, w, *refs):
+    lane = me[0]
+    blocks = refs[: len(steps)]
+    olds = refs[len(steps) : -3]
+    keys, values, query = refs[-3:]
+    rows, ch = keys.shape
+    n = query.shape[0]
+    width = blocks[0].shape[1]
+    own = pl.multiple_of((lane % 2) * n, 16)
+    parts = [scaled(b, gain, lane, k, rows) for b, k in zip(blocks, steps)]
+    owns = [
+        (b[pl.ds(own, n), :].astype(F32) * gain[lane ^ k]).astype(BF16)
+        for b, k in zip(blocks, steps)
+    ]
+    for i, (first, out, use) in enumerate(
+        ((ch, keys, parts), (2 * ch, values, parts), (0, query, owns))
+    ):
+        acc = olds[i][...] if olds else None
+        for k, part in zip(steps, use):
+            at = pl.multiple_of((lane ^ k) * width, width)
+            term = jnp.dot(part, w[pl.ds(at, width), first : first + ch], preferred_element_type=F32)
+            acc = term if acc is None else acc + term
+        out[...] = acc
+
+
+def project(me, steps, blocks, gain, w, n, olds=()):
+    rows = 2 * n
+    ch, width = w.shape[0], blocks[0].shape[1]
+    return pl.pallas_call(
+        functools.partial(project_kernel, steps),
+        out_shape=(vout((rows, ch), F32), vout((rows, ch), F32), vout((n, ch), F32)),
+        in_specs=[sspec()] + [vspec()] * (2 + len(blocks) + len(olds)),
+        out_specs=(vspec(),) * 3,
+        input_output_aliases={3 + len(blocks) + i: i for i in range(len(olds))},
+        compiler_params=pltpu.CompilerParams(vmem_limit_bytes=16 << 20),
+        cost_estimate=pl.CostEstimate(
+            flops=2 * (2 * rows + n) * width * len(blocks) * ch,
+            bytes_accessed=6 * ch * width * len(blocks),
+            transcendentals=0,
+        ),
+        name="project",
+    )(me, gain, w, *blocks, *olds)
+
+
 def attend_kernel(
-    me, b0, b1, b2, b3, gain, w, k_far, v_far, bias_y, bias_d, w_out, out, keys, values, query, attended
+    steps, me, b0, b1, b2, b3, gain, w, key_sum, value_sum, query_sum, k_far, v_far, bias_y, bias_d,
+    w_out, out, keys, values, query, attended
 ):
     lane = me[0]
     core = lane % 2
@@ -276,14 +329,28 @@
     width = b0.shape[1]
     hd = ch // H
     blocks = (b0, b1, b2, b3)
-    parts = normed_of(blocks, gain, lane, ch, rows)
-    for first, dst in ((ch, keys), (2 * ch, values), (0, query)):
-        acc = None
-        for k, part in enumerate(parts):
-            at = pl.multiple_of((lane ^ k) * width, width)
-            term = jnp.dot(part, w[pl.ds(at, width), first : first + ch], preferred_element_type=F32)
-            acc = term if acc is None else acc + term
-        dst[0:rows, :] = acc.astype(BF16)
+    own = pl.multiple_of(core * n, 16)
+
+    def factor_of(at, count):
+        square = 0.0
+        for b in blocks:
+            stream = b[pl.ds(at, count), :].astype(F32)
+            square = square + jnp.sum(stream * stream, axis=-1, keepdims=True)
+        return lax.rsqrt(square * (1.0 / ch) + 1e-06)
+
+    for first, dst, acc, at, count in (
+        (0, query, query_sum, own, n),
+        (ch, keys, key_sum, 0, rows),
+        (2 * ch, values, value_sum, 0, rows),
+    ):
+        total = acc[...]
+        for k in steps:
+            part = (blocks[k][pl.ds(at, count), :].astype(F32) * gain[lane ^ k]).astype(BF16)
+            place = pl.multiple_of((lane ^ k) * width, width)
+            total = total + jnp.dot(
+                part, w[pl.ds(place, width), first : first + ch], preferred_element_type=F32
+            )
+        dst[0:count, :] = (total * factor_of(at, count)).astype(BF16)
     keys[rows : 2 * rows, :] = k_far[...]
     values[rows : 2 * rows, :] = v_far[...]
     pieces = []
@@ -291,12 +358,11 @@
         a, c = (v[rows : rows + H, 0:n].astype(F32) for v in (a, c))
         pieces += [jnp.where(core == 0, a, c), jnp.where(core == 0, c, a)]
     bias = jnp.concatenate(pieces, axis=1)
-    own = pl.multiple_of(core * n, 16)
     group = 256 // hd
     head_of = lax.broadcasted_iota(jnp.int32, (n, 256), 1) // hd
     for g in range(ch // 256):
         cols = slice(g * 256, (g + 1) * 256)
-        q = query[pl.ds(own, n), cols] * jnp.asarray(1.0 / math.sqrt(hd), BF16)
+        q = query[:, cols] * jnp.asarray(1.0 / math.sqrt(hd), BF16)
         stacked = jnp.concatenate(
             [jnp.where(head_of == t, q, jnp.zeros_like(q)) for t in range(group)], axis=0
         )
@@ -321,28 +387,28 @@
         out[:, pl.ds(at, width)] = mixed.astype(BF16)
 
 
-def attend(me, blocks, gain, w, k_far, v_far, bias_y, bias_d, w_out):
+def attend(me, steps, blocks, gain, w, sums, k_far, v_far, bias_y, bias_d, w_out):
     rows, ch = k_far.shape
     n = rows // 2
     return pl.pallas_call(
-        attend_kernel,
+        functools.partial(attend_kernel, steps),
         out_shape=jax.ShapeDtypeStruct((n, ch), BF16),
-        in_specs=[sspec()] + [vspec()] * 11,
+        in_specs=[sspec()] + [vspec()] * 14,
         out_specs=vspec(),
         scratch_shapes=[
             VMEM((2 * rows, ch), BF16),
             VMEM((2 * rows, ch), BF16),
-            VMEM((rows, ch), BF16),
+            VMEM((n, ch), BF16),
             VMEM((n, ch), BF16),
         ],
-        compiler_params=pltpu.CompilerParams(vmem_limit_bytes=40 << 20),
+        compiler_params=pltpu.CompilerParams(vmem_limit_bytes=32 << 20),
         cost_estimate=pl.CostEstimate(
-            flops=2 * rows * ch * 3 * ch + 4 * n * 2 * rows * ch * 4,
+            flops=2 * rows * ch * ch + 4 * n * 2 * rows * ch * 4,
             bytes_accessed=8 * ch * ch,
             transcendentals=n * 2 * rows * H,
         ),
         name="attend",
-    )(me, *blocks, gain, w, k_far, v_far, bias_y, bias_d, w_out)
+    )(me, *blocks, gain, w, *sums, k_far, v_far, bias_y, bias_d, w_out)
 
 
 def four_shard_device(fields, conv_weight, norm_gain, qkv_weight, out_weight, key_bias):
@@ -350,7 +416,7 @@
     width = conv_weight.shape[1]
     lane = lax.axis_index("lon")
     core = lane % 2
-    me = jnp.stack([lane, lax.axis_index("lat")]).astype(jnp.int32)
+    me = jnp.stack([lane, lax.axis_index("lat"), lax.axis_size("lat")]).astype(jnp.int32)
     lon_size = lax.axis_size("lon")
     lat_size = lax.axis_size("lat")
 
@@ -358,8 +424,17 @@
         return lax.ppermute(value, "lon", [(i, i ^ bit) for i in range(lon_size)])
 
     def lat_swap(value, first):
-        pairs = [(i, i + 1) for i in range(first, lat_size - 1, 2)]
-        return lax.ppermute(value, "lat", pairs + [(b, a) for a, b in pairs])
+        def target(i):
+            j = i + 1 if (i - first) % 2 == 0 else i - 1
+            return j if 0 <= j < lat_size else i
+
+        pairs = []
+        for m in range(lon_size):
+            for i in range(lat_size):
+                j = target(i)
+                to = (m, j) if j != i else (m ^ 1, i)
+                pairs.append((m * lat_size + i, to[0] * lat_size + to[1]))
+        return lax.ppermute(value, ("lon", "lat"), pairs)
 
     x = fields.reshape(n, ch)
     edge = lax.dynamic_slice_in_dim(x, core * (n - EDGE), EDGE, axis=0)
@@ -387,7 +462,12 @@
 
     gain = norm_gain.reshape(lon_size, 1, width)
     k_far, v_far = keys_of(me, (far, far_c, far_y, far_d), gain, qkv_weight)
-    out = attend(me, (near, near_c, near_y, near_d), gain, qkv_weight, k_far, v_far, far_y, far_d, out_weight)
+    sums = project(me, (0, 1), (near, near_c), gain, qkv_weight, n)
+    sums = project(me, (2,), (near_y,), gain, qkv_weight, n, sums)
+    out = attend(
+        me, (3,), (near, near_c, near_y, near_d), gain, qkv_weight, sums, k_far, v_far, far_y,
+        far_d, out_weight
+    )
     return out.reshape(fields.shape)
 
 

time: 56.5 us -> 53.7 us (0.950)
  starting transfers between devices: 16.4 us -> 13.8 us
  Pallas kernels: 20.3 us -> 21.8 us
  waiting for transfers between devices: 18.1 us -> 16.9 us
    ppermute x4, starting transfers between devices: 7.95 us -> 5.09 us  [lat_swap(): return lax.ppermute(value, ('lon', 'lat'), pairs)]
    ppermute x11, waiting for transfers between devices: 16.2 us -> 14.4 us  [swap(): return lax.ppermute(value, 'lon', [(i, i ^ bit) for i in range(lon_size)])]
    pallas_call x1 -> x3, Pallas kernels: 8.58 us -> 10.2 us  [the longest x1 6.84 us: attend(): pl.pallas_call(functools.partial(attend_kernel, steps), out_shape=jax.Sha...]
    ppermute x4, waiting for transfers between devices: 1.86 us -> 2.49 us  [lat_swap(): return lax.ppermute(value, ('lon', 'lat'), pairs)]
  transfers between devices with their start and end apart: 15 -> 15, of which waited for: 5 -> 5; matrix products, arithmetic and copies ran while one was open for 2% -> 2% of each run, Pallas kernels for 21% -> 28%
where the time goes in v1:
time: 53.7 us; the launch traced here: 53.5 us
  Pallas kernels  21.8 us (41%)
  waiting for transfers between devices  16.9 us (31%)
  starting transfers between devices  13.8 us (26%)
  local copies, waits for them, and re-layouts  0.79 us (1%)
    ppermute x11, waiting for transfers between devices, swap(): return lax.ppermute(value, 'lon', [(i, i ^ bit) for i in range(lon_size)])  14.4 us
    ppermute x11, starting transfers between devices, swap(): return lax.ppermute(value, 'lon', [(i, i ^ bit) for i in range(lon_size)])  8.67 us
    pallas_call x1, Pallas kernels, attend(): pl.pallas_call(functools.partial(attend_kernel, steps), out_shape=jax.Sha...  6.84 us
    pallas_call x2, Pallas kernels, conv_half(): pl.pallas_call(conv_kernel, out_shape=(vout((2 * n, width), BF16), vout((...  5.17 us
    ppermute x4, starting transfers between devices, lat_swap(): return lax.ppermute(value, ('lon', 'lat'), pairs)  5.09 us
    pallas_call x2, Pallas kernels, project(): pl.pallas_call(functools.partial(project_kernel, steps), out_shape=(vout(...  3.32 us
    pallas_call x1, Pallas kernels, load(): pl.pallas_call(load_kernel, out_shape=tuple((vout(a.shape, a.dtype) for a...  2.57 us
    pallas_call x1, Pallas kernels, keys_of(): pl.pallas_call(keys_kernel, out_shape=(out, out), in_specs=[sspec()] + [v...  2.51 us
  transfers between devices with their start and end apart: 15, of which 5 were waited for; matrix products, arithmetic and copies ran while one was open for 2% of the time, Pallas kernels for 28%

profile of v1, /device:TPU:0, one launch (start us, length us, event | category | flops | bytes accessed | tf_op | source)
XLA Modules:
  0.0 53.5 jit_solution(15101262710138187748)
XLA Ops:
  0.0 3.0 %collective-permute-start.6 = (bf16[192,1024]{1,0:T(8,128)(2,1)}, bf16[192,1024]{1,0:T(8,128)(2,1)S(1)}, u32[]{:S(2)}, u32[]{:S(2)}) collective-permute-start(bf16[192,1024]{1,0:T(8,128)(2,1)} %bitcast.16), channel_id=1, source_target_pairs={{0,8},{4,12},{8,0},{12,4},{1,9},{5,13},{9,1},{13,5},{2,10},{6,14},... | collective-permute-start | bytes 1179656 | tf_op jit(solution)/shard_map/ppermute | solution.py:424
  3.0 0.0 collective-permute-start
  3.0 9.3 %collective-permute-done.6.xa = bf16[192,1024]{1,0:T(8,128)(2,1)S(1)} collective-permute-done((bf16[192,1024]{1,0:T(8,128)(2,1)}, bf16[192,1024]{1,0:T(8,128)(2,1)S(1)}, u32[]{:S(2)}, u32[]{:S(2)}) %collective-permute-start.6) | collective-permute-done | bytes 393248 | tf_op jit(solution)/shard_map/ppermute | solution.py:424
  12.3 0.0 collective-permute-start.7
  12.3 0.8 %dynamic-slice_bitcast_fusion = bf16[16,1024]{1,0:T(8,128)(2,1)S(1)} fusion(bf16[1,192,1024]{2,1,0:T(8,128)(2,1)} %param.6, s32[]{:T(128)S(6)} %select_n.11), kind=kLoop, calls=%fused_computation | loop fusion | bytes 65540 | tf_op jit(solution)/shard_map/dynamic_slice | solution.py:440
  13.1 1.7 %collective-permute-start.1 = (bf16[16,1024]{1,0:T(8,128)(2,1)S(1)}, bf16[16,1024]{1,0:T(8,128)(2,1)S(1)}, u32[]{:S(2)}, u32[]{:S(2)}) collective-permute-start(bf16[16,1024]{1,0:T(8,128)(2,1)S(1)} %dynamic-slice_bitcast_fusion), channel_id=1, source_target_pairs={{0,8},{4,12},{8,0},{12,4},{1,9},{5,13},{9,1},{13,5},{2,10},{6,14},... | collective-permute-start | bytes 98312 | tf_op jit(solution)/shard_map/ppermute | solution.py:424
  14.8 2.2 %collective-permute-done.1.ea = bf16[16,1024]{1,0:T(8,128)(2,1)S(1)} collective-permute-done((bf16[16,1024]{1,0:T(8,128)(2,1)S(1)}, bf16[16,1024]{1,0:T(8,128)(2,1)S(1)}, u32[]{:S(2)}, u32[]{:S(2)}) %collective-permute-start.1) | collective-permute-done | bytes 32800 | tf_op jit(solution)/shard_map/ppermute | solution.py:424
  17.0 0.0 collective-permute-start.2
  17.0 0.1 pad_add_fusion.me
  17.1 2.6 %load.1 = (bf16[192,1024]{1,0:T(8,128)(2,1)S(1)}, bf16[9216,256]{1,0:T(8,128)(2,1)S(1)}) custom-call(bf16[192,1024]{1,0:T(8,128)(2,1)} %bitcast.18, bf16[9216,256]{1,0:T(8,128)(2,1)} %refs_1_.1), custom_call_target="tpu_custom_call" | custom-call | bytes 5111808 | tf_op jit(solution)/shard_map/load/pallas_call | solution.py:144
  19.7 0.0 collective-permute-done.2.eb
  19.7 0.0 slice-start
  19.7 2.6 %conv_half.2 = (bf16[384,256]{1,0:T(8,128)(2,1)S(1)}, bf16[384,256]{1,0:T(8,128)(2,1)S(1)}, f32[384,256]{1,0:T(8,128)S(1)}) custom-call(s32[3]{0:T(128)S(1)} %pad_add_fusion.me, bf16[192,1024]{1,0:T(8,128)(2,1)S(1)} %get-tuple-element.21.xa.ea, bf16[192,1024]{1,0:T(8,128)(2,1)S(1)} %collective-permute-done.xb.eb, ...), custom_call_target="tpu_custom_call" | custom-call | flops 1811939328 | bytes 4718592 | tf_op jit(solution)/shard_map/conv_half/pallas_call | solution.py:180
  22.3 1.9 %collective-permute-start.3 = (bf16[384,256]{1,0:T(8,128)(2,1)S(1)}, bf16[384,256]{1,0:T(8,128)(2,1)S(1)}, u32[]{:S(2)}, u32[]{:S(2)}) collective-permute-start(bf16[384,256]{1,0:T(8,128)(2,1)S(1)} %get-tuple-element.23), channel_id=1, source_target_pairs={{0,1},{1,0},{2,3},{3,2},{4,5},{5,4},{6,7},{7,6},{8,9},{9,8},{10,11... | collective-permute-start | bytes 589832 | tf_op jit(solution)/shard_map/ppermute | solution.py:437
  24.2 0.2 collective-permute-start.4
  24.4 2.6 %conv_half.3 = (bf16[384,256]{1,0:T(8,128)(2,1)S(1)}, bf16[384,256]{1,0:T(8,128)(2,1)S(1)}, f32[384,256]{1,0:T(8,128)S(1)}) custom-call(s32[3]{0:T(128)S(1)} %pad_add_fusion.me, bf16[192,1024]{1,0:T(8,128)(2,1)S(1)} %collective-permute-done.6.xa, bf16[192,1024]{1,0:T(8,128)(2,1)S(1)} %collective-permute-done.7.xb, ...), custom_call_target="tpu_custom_call" | custom-call | flops 1811939328 | bytes 4718592 | tf_op jit(solution)/shard_map/conv_half/pallas_call | solution.py:180
  27.0 0.0 copy-start.1
  27.0 3.0 %collective-permute-start.8 = (bf16[384,256]{1,0:T(8,128)(2,1)S(1)}, bf16[384,256]{1,0:T(8,128)(2,1)S(1)}, u32[]{:S(2)}, u32[]{:S(2)}) collective-permute-start(bf16[384,256]{1,0:T(8,128)(2,1)S(1)} %get-tuple-element.26), channel_id=1, source_target_pairs={{0,1},{1,0},{2,3},{3,2},{4,5},{5,4},{6,7},{7,6},{8,9},{9,8},{10,11... | collective-permute-start | bytes 589832 | tf_op jit(solution)/shard_map/ppermute | solution.py:437
  30.0 0.7 %residual_of.2.refs_0_.b0 = bf16[400,256]{1,0:T(8,128)(2,1)S(1)} custom-call(s32[3]{0:T(128)S(1)} %pad_add_fusion.me, bf16[384,256]{1,0:T(8,128)(2,1)S(1)} %collective-permute-done.3.first, bf16[384,256]{1,0:T(8,128)(2,1)S(1)} %collective-permute-done.4.second, f32[384,256]{1,0:T(8,128)S(1)} %get-tuple-element.25.mid, ...), custom_call_target="tpu_custom_call" | custom-call | flops 409600 | bytes 819200 | tf_op jit(solution)/shard_map/residual_of/pallas_call | solution.py:222
  30.7 1.6 %collective-permute-start.13 = (bf16[400,256]{1,0:T(8,128)(2,1)S(1)}, bf16[400,256]{1,0:T(8,128)(2,1)S(1)}, u32[]{:S(2)}, u32[]{:S(2)}) collective-permute-start(bf16[400,256]{1,0:T(8,128)(2,1)S(1)} %residual_of.2.refs_0_.b0), channel_id=1, source_target_pairs={{0,8},{4,12},{8,0},{12,4},{1,9},{5,13},{9,1},{13,5},{2,10},{6,14},... | collective-permute-start | bytes 614408 | tf_op jit(solution)/shard_map/ppermute | solution.py:424
  32.3 0.2 collective-permute-start.5
  32.5 2.5 %collective-permute-done.8.first = bf16[384,256]{1,0:T(8,128)(2,1)S(1)} collective-permute-done((bf16[384,256]{1,0:T(8,128)(2,1)S(1)}, bf16[384,256]{1,0:T(8,128)(2,1)S(1)}, u32[]{:S(2)}, u32[]{:S(2)}) %collective-permute-start.8) | collective-permute-done | bytes 196640 | tf_op jit(solution)/shard_map/ppermute | solution.py:437
  35.0 0.7 %residual_of.3.b0 = bf16[384,256]{1,0:T(8,128)(2,1)S(1)} custom-call(s32[3]{0:T(128)S(1)} %pad_add_fusion.me, bf16[384,256]{1,0:T(8,128)(2,1)S(1)} %collective-permute-done.8.first, bf16[384,256]{1,0:T(8,128)(2,1)S(1)} %collective-permute-done.9.second, f32[384,256]{1,0:T(8,128)S(1)} %get-tuple-element.28.mid, ...), custom_call_target="tpu_custom_call" | custom-call | flops 393216 | bytes 786432 | tf_op jit(solution)/shard_map/residual_of/pallas_call | solution.py:222
  35.7 1.6 %collective-permute-start.10 = (bf16[384,256]{1,0:T(8,128)(2,1)S(1)}, bf16[384,256]{1,0:T(8,128)(2,1)S(1)}, u32[]{:S(2)}, u32[]{:S(2)}) collective-permute-start(bf16[384,256]{1,0:T(8,128)(2,1)S(1)} %residual_of.3.b0), channel_id=1, source_target_pairs={{0,8},{4,12},{8,0},{12,4},{1,9},{5,13},{9,1},{13,5},{2,10},{6,14},... | collective-permute-start | bytes 589832 | tf_op jit(solution)/shard_map/ppermute | solution.py:424
  37.3 1.4 %collective-permute-done.13.b2.bias_y = bf16[400,256]{1,0:T(8,128)(2,1)S(1)} collective-permute-done((bf16[400,256]{1,0:T(8,128)(2,1)S(1)}, bf16[400,256]{1,0:T(8,128)(2,1)S(1)}, u32[]{:S(2)}, u32[]{:S(2)}) %collective-permute-start.13) | collective-permute-done | bytes 204832 | tf_op jit(solution)/shard_map/ppermute | solution.py:424
  38.7 0.5 collective-permute-start.12
  39.3 1.7 %project.2 = (f32[384,1024]{1,0:T(8,128)S(1)}, f32[384,1024]{1,0:T(8,128)S(1)}, f32[192,1024]{1,0:T(8,128)S(1)}) custom-call(s32[3]{0:T(128)S(1)} %pad_add_fusion.me, f32[4,1,256]{2,1,0:T(1,128)S(1)} %bitcast.12, bf16[1024,3072]{1,0:T(8,128)(2,1)S(1)} %bitcast.11, bf16[400,256]{1,0:T(8,128)(2,1)S(1)} %residual_of.2.refs_0_.b0, ...), custom_call_target="tpu_custom_call" | custom-call | flops 1006632960 | bytes 3145728 | tf_op jit(solution)/shard_map/project/pallas_call | solution.py:305
  41.0 1.5 %collective-permute-done.10.refs_0_.b2 = bf16[384,256]{1,0:T(8,128)(2,1)S(1)} collective-permute-done((bf16[384,256]{1,0:T(8,128)(2,1)S(1)}, bf16[384,256]{1,0:T(8,128)(2,1)S(1)}, u32[]{:S(2)}, u32[]{:S(2)}) %collective-permute-start.10) | collective-permute-done | bytes 196640 | tf_op jit(solution)/shard_map/ppermute | solution.py:424
  42.5 1.6 %project.3 = (f32[384,1024]{1,0:T(8,128)S(1)}, f32[384,1024]{1,0:T(8,128)S(1)}, f32[192,1024]{1,0:T(8,128)S(1)}) custom-call(s32[3]{0:T(128)S(1)} %pad_add_fusion.me, f32[4,1,256]{2,1,0:T(1,128)S(1)} %bitcast.13, bf16[1024,3072]{1,0:T(8,128)(2,1)S(1)} %bitcast.11, ...), custom_call_target="tpu_custom_call", output_to_operand_aliasing={{0}: (4, {}), {1}: (5, {}), {2}: (6, {})} | custom-call | flops 503316480 | bytes 1572864 | tf_op jit(solution)/shard_map/project/pallas_call | solution.py:305
  44.1 0.0 copy-start
  44.1 2.5 %keys_of.1 = (bf16[384,1024]{1,0:T(8,128)(2,1)S(1)}, bf16[384,1024]{1,0:T(8,128)(2,1)S(1)}) custom-call(s32[3]{0:T(128)S(1)} %pad_add_fusion.me, bf16[384,256]{1,0:T(8,128)(2,1)S(1)} %residual_of.3.b0, bf16[384,256]{1,0:T(8,128)(2,1)S(1)} %collective-permute-done.12.b1, bf16[400,256]{1,0:T(8,128)(2,1)S(1)} %collective-permute-done.13.b2.bias_y, ...), custom_call_target="tpu_custom_call" | custom-call | flops 1610612736 | bytes 4194304 | tf_op jit(solution)/shard_map/keys_of/pallas_call | solution.py:260
  46.6 6.8 %attend.1 = bf16[192,1024]{1,0:T(8,128)(2,1)} custom-call(s32[3]{0:T(128)S(1)} %pad_add_fusion.me, bf16[400,256]{1,0:T(8,128)(2,1)S(1)} %residual_of.2.refs_0_.b0, bf16[400,256]{1,0:T(8,128)(2,1)S(1)} %collective-permute-done.5.refs_1_.b1, bf16[384,256]{1,0:T(8,128)(2,1)S(1)} %collective-permute-done.10.refs_0_.b2, ...), custom_call_target="tpu_custom_call" | custom-call | flops 3221225472 | bytes 8388608 | tf_op jit(solution)/shard_map/attend/pallas_call | solution.py:393
  (21 shorter events, 0.1 us)
Async XLA Ops:
  0.0 12.3 %collective-permute-start.6 = (bf16[192,1024]{1,0:T(8,128)(2,1)}, bf16[192,1024]{1,0:T(8,128)(2,1)S(1)}, u32[]{:S(2)}, u32[]{:S(2)}) collective-permute-start(bf16[192,1024]{1,0:T(8,128)(2,1)} %bitcast.16), channel_id=1, source_target_pairs={{0,8},{4,12},{8,0},{12,4},{1,9},{5,13},{9,1},{13,5},{2,10},{6,14},... | collective-permute-start | bytes 1179656 | tf_op jit(solution)/shard_map/ppermute | solution.py:424
  3.0 16.7 %collective-permute-start = (bf16[192,1024]{1,0:T(8,128)(2,1)}, bf16[192,1024]{1,0:T(8,128)(2,1)S(1)}, u32[]{:S(2)}, u32[]{:S(2)}) collective-permute-start(bf16[192,1024]{1,0:T(8,128)(2,1)} %bitcast.17), channel_id=1, source_target_pairs={{0,4},{4,0},{8,12},{12,8},{1,5},{5,1},{9,13},{13,9},{2,6},{6,2},{1... | collective-permute-start | bytes 1179656 | tf_op jit(solution)/shard_map/ppermute | solution.py:424
  12.3 12.1 %collective-permute-start.7 = (bf16[192,1024]{1,0:T(8,128)(2,1)S(1)}, bf16[192,1024]{1,0:T(8,128)(2,1)S(1)}, u32[]{:S(2)}, u32[]{:S(2)}) collective-permute-start(bf16[192,1024]{1,0:T(8,128)(2,1)S(1)} %collective-permute-done.6.xa), channel_id=1, source_target_pairs={{0,4},{4,0},{8,12},{12,8},{1,5},{5,1},{9,13},{13,9},{2,6},{6,2},{1... | collective-permute-start | bytes 1179656 | tf_op jit(solution)/shard_map/ppermute | solution.py:424
  13.1 3.9 %collective-permute-start.1 = (bf16[16,1024]{1,0:T(8,128)(2,1)S(1)}, bf16[16,1024]{1,0:T(8,128)(2,1)S(1)}, u32[]{:S(2)}, u32[]{:S(2)}) collective-permute-start(bf16[16,1024]{1,0:T(8,128)(2,1)S(1)} %dynamic-slice_bitcast_fusion), channel_id=1, source_target_pairs={{0,8},{4,12},{8,0},{12,4},{1,9},{5,13},{9,1},{13,5},{2,10},{6,14},... | collective-permute-start | bytes 98312 | tf_op jit(solution)/shard_map/ppermute | solution.py:424
  17.0 2.7 %collective-permute-start.2 = (bf16[16,1024]{1,0:T(8,128)(2,1)S(1)}, bf16[16,1024]{1,0:T(8,128)(2,1)S(1)}, u32[]{:S(2)}, u32[]{:S(2)}) collective-permute-start(bf16[16,1024]{1,0:T(8,128)(2,1)S(1)} %collective-permute-done.1.ea), channel_id=1, source_target_pairs={{0,4},{4,0},{8,12},{12,8},{1,5},{5,1},{9,13},{13,9},{2,6},{6,2},{1... | collective-permute-start | bytes 98312 | tf_op jit(solution)/shard_map/ppermute | solution.py:424
  19.7 19.5 %slice-start = ((s8[6291456]{0:T(1024)(128)(4,1)}), s8[4194304]{0:T(1024)(128)(4,1)S(1)}, s32[]{:S(2)}) async-start(s8[6291456]{0:T(1024)(128)(4,1)} %bitcast.10), calls=%async_computation | async-start | bytes 8388608
  22.3 7.7 %collective-permute-start.3 = (bf16[384,256]{1,0:T(8,128)(2,1)S(1)}, bf16[384,256]{1,0:T(8,128)(2,1)S(1)}, u32[]{:S(2)}, u32[]{:S(2)}) collective-permute-start(bf16[384,256]{1,0:T(8,128)(2,1)S(1)} %get-tuple-element.23), channel_id=1, source_target_pairs={{0,1},{1,0},{2,3},{3,2},{4,5},{5,4},{6,7},{7,6},{8,9},{9,8},{10,11... | collective-permute-start | bytes 589832 | tf_op jit(solution)/shard_map/ppermute | solution.py:437
  24.1 5.8 %copy-start.2 = (bf16[1,192,16]{1,2,0:T(8,128)(2,1)S(1)}, bf16[1,192,16]{1,2,0:T(8,128)(2,1)}, u32[]{:S(2)}) copy-start(bf16[1,192,16]{1,2,0:T(8,128)(2,1)} %param.11) | copy-start | bytes 18436
  24.2 15.1 %slice-start.1 = ((s8[6291456]{0:T(1024)(128)(4,1)}), s8[2097152]{0:T(1024)(128)(4,1)S(1)}, s32[]{:S(2)}) async-start(s8[6291456]{0:T(1024)(128)(4,1)} %bitcast.10), calls=%async_computation.1 | async-start | bytes 4194304
  24.2 5.9 %collective-permute-start.4 = (bf16[384,256]{1,0:T(8,128)(2,1)S(1)}, bf16[384,256]{1,0:T(8,128)(2,1)S(1)}, u32[]{:S(2)}, u32[]{:S(2)}) collective-permute-start(bf16[384,256]{1,0:T(8,128)(2,1)S(1)} %get-tuple-element.24), channel_id=1, source_target_pairs={{0,4},{1,2},{2,1},{3,7},{4,0},{5,6},{6,5},{7,3},{8,12},{9,10},{10,... | collective-permute-start | bytes 589832 | tf_op jit(solution)/shard_map/ppermute | solution.py:437
  27.0 12.3 %copy-start.1 = (f32[1024]{0:T(1024)S(1)}, f32[1024]{0:T(1024)}, u32[]{:S(2)}) copy-start(f32[1024]{0:T(1024)} %param.8) | copy-start | bytes 12292
  27.0 8.0 %collective-permute-start.8 = (bf16[384,256]{1,0:T(8,128)(2,1)S(1)}, bf16[384,256]{1,0:T(8,128)(2,1)S(1)}, u32[]{:S(2)}, u32[]{:S(2)}) collective-permute-start(bf16[384,256]{1,0:T(8,128)(2,1)S(1)} %get-tuple-element.26), channel_id=1, source_target_pairs={{0,1},{1,0},{2,3},{3,2},{4,5},{5,4},{6,7},{7,6},{8,9},{9,8},{10,11... | collective-permute-start | bytes 589832 | tf_op jit(solution)/shard_map/ppermute | solution.py:437
  30.0 5.0 %collective-permute-start.9 = (bf16[384,256]{1,0:T(8,128)(2,1)S(1)}, bf16[384,256]{1,0:T(8,128)(2,1)S(1)}, u32[]{:S(2)}, u32[]{:S(2)}) collective-permute-start(bf16[384,256]{1,0:T(8,128)(2,1)S(1)} %get-tuple-element.27), channel_id=1, source_target_pairs={{0,4},{1,2},{2,1},{3,7},{4,0},{5,6},{6,5},{7,3},{8,12},{9,10},{10,... | collective-permute-start | bytes 589832 | tf_op jit(solution)/shard_map/ppermute | solution.py:437
  30.7 8.0 %collective-permute-start.13 = (bf16[400,256]{1,0:T(8,128)(2,1)S(1)}, bf16[400,256]{1,0:T(8,128)(2,1)S(1)}, u32[]{:S(2)}, u32[]{:S(2)}) collective-permute-start(bf16[400,256]{1,0:T(8,128)(2,1)S(1)} %residual_of.2.refs_0_.b0), channel_id=1, source_target_pairs={{0,8},{4,12},{8,0},{12,4},{1,9},{5,13},{9,1},{13,5},{2,10},{6,14},... | collective-permute-start | bytes 614408 | tf_op jit(solution)/shard_map/ppermute | solution.py:424
  32.3 6.9 %collective-permute-start.5 = (bf16[400,256]{1,0:T(8,128)(2,1)S(1)}, bf16[400,256]{1,0:T(8,128)(2,1)S(1)}, u32[]{:S(2)}, u32[]{:S(2)}) collective-permute-start(bf16[400,256]{1,0:T(8,128)(2,1)S(1)} %residual_of.2.refs_0_.b0), channel_id=1, source_target_pairs={{0,4},{4,0},{8,12},{12,8},{1,5},{5,1},{9,13},{13,9},{2,6},{6,2},{1... | collective-permute-start | bytes 614408 | tf_op jit(solution)/shard_map/ppermute | solution.py:424
  35.7 6.8 %collective-permute-start.10 = (bf16[384,256]{1,0:T(8,128)(2,1)S(1)}, bf16[384,256]{1,0:T(8,128)(2,1)S(1)}, u32[]{:S(2)}, u32[]{:S(2)}) collective-permute-start(bf16[384,256]{1,0:T(8,128)(2,1)S(1)} %residual_of.3.b0), channel_id=1, source_target_pairs={{0,8},{4,12},{8,0},{12,4},{1,9},{5,13},{9,1},{13,5},{2,10},{6,14},... | collective-permute-start | bytes 589832 | tf_op jit(solution)/shard_map/ppermute | solution.py:424
  38.7 5.4 %collective-permute-start.14 = (bf16[400,256]{1,0:T(8,128)(2,1)S(1)}, bf16[400,256]{1,0:T(8,128)(2,1)S(1)}, u32[]{:S(2)}, u32[]{:S(2)}) collective-permute-start(bf16[400,256]{1,0:T(8,128)(2,1)S(1)} %collective-permute-done.13.b2.bias_y), channel_id=1, source_target_pairs={{0,4},{4,0},{8,12},{12,8},{1,5},{5,1},{9,13},{13,9},{2,6},{6,2},{1... | collective-permute-start | bytes 614408 | tf_op jit(solution)/shard_map/ppermute | solution.py:424
  38.7 5.4 %collective-permute-start.12 = (bf16[384,256]{1,0:T(8,128)(2,1)S(1)}, bf16[384,256]{1,0:T(8,128)(2,1)S(1)}, u32[]{:S(2)}, u32[]{:S(2)}) collective-permute-start(bf16[384,256]{1,0:T(8,128)(2,1)S(1)} %residual_of.3.b0), channel_id=1, source_target_pairs={{0,4},{4,0},{8,12},{12,8},{1,5},{5,1},{9,13},{13,9},{2,6},{6,2},{1... | collective-permute-start | bytes 589832 | tf_op jit(solution)/shard_map/ppermute | solution.py:424
  42.5 4.2 %collective-permute-start.11 = (bf16[384,256]{1,0:T(8,128)(2,1)S(1)}, bf16[384,256]{1,0:T(8,128)(2,1)S(1)}, u32[]{:S(2)}, u32[]{:S(2)}) collective-permute-start(bf16[384,256]{1,0:T(8,128)(2,1)S(1)} %collective-permute-done.10.refs_0_.b2), channel_id=1, source_target_pairs={{0,4},{4,0},{8,12},{12,8},{1,5},{5,1},{9,13},{13,9},{2,6},{6,2},{1... | collective-permute-start | bytes 589832 | tf_op jit(solution)/shard_map/ppermute | solution.py:424
  44.1 2.6 %copy-start = (bf16[1024,1024]{1,0:T(8,128)(2,1)S(1)}, bf16[1024,1024]{1,0:T(8,128)(2,1)}, u32[]{:S(2)}) copy-start(bf16[1024,1024]{1,0:T(8,128)(2,1)} %w_out.1) | copy-start | bytes 6291460

commit v2 on v1

--- a/solution.py
+++ b/solution.py
@@ -122,46 +122,54 @@
     return VMEM(shape, dtype)
 
 
-def load_kernel(*refs):
+def load_kernel(pieces, *refs):
     count = (len(refs) - 1) // 2
     sem = refs[-1]
     copies = []
-    for src, dst in zip(refs[:count], refs[count : 2 * count]):
-        rows = src.shape[0]
-        pieces = PIECES if rows % (16 * PIECES) == 0 else 1
-        size = rows // pieces
-        for p in range(pieces):
-            at = pl.ds(p * size, size)
-            copy = pltpu.make_async_copy(src.at[at], dst.at[at], sem.at[len(copies)])
+    for src, dst, parts in zip(refs[:count], refs[count : 2 * count], pieces):
+        place = 0
+        for start, size in parts:
+            copy = pltpu.make_async_copy(
+                src.at[pl.ds(start, size)], dst.at[pl.ds(place, size)], sem.at[len(copies)]
+            )
             copy.start()
             copies.append(copy)
+            place += size
     for copy in copies:
         copy.wait()
 
 
-def load(*arrays):
-    total = sum(a.size * a.dtype.itemsize for a in arrays)
-    return pl.pallas_call(
-        load_kernel,
-        out_shape=tuple(vout(a.shape, a.dtype) for a in arrays),
+def load(arrays, ranges):
+    pieces, shapes = [], []
+    for a, spans in zip(arrays, ranges):
+        parts = []
+        for start, size in spans:
+            cut = size // PIECES if size % (16 * PIECES) == 0 else size
+            parts += [(start + at, cut) for at in range(0, size, cut)]
+        pieces.append(tuple(parts))
+        shapes.append(vout((sum(size for _, size in spans),) + a.shape[1:], a.dtype))
+    total = sum(math.prod(v.shape) * 2 for v in shapes)
+    return pl.pallas_call(
+        functools.partial(load_kernel, tuple(pieces)),
+        out_shape=tuple(shapes),
         in_specs=[aspec()] * len(arrays),
         out_specs=tuple(vspec() for _ in arrays),
-        scratch_shapes=[pltpu.SemaphoreType.DMA((PIECES * len(arrays),))],
+        scratch_shapes=[pltpu.SemaphoreType.DMA((sum(len(p) for p in pieces),))],
         compiler_params=pltpu.CompilerParams(vmem_limit_bytes=1 << 20),
         cost_estimate=pl.CostEstimate(flops=0, bytes_accessed=total, transcendentals=0),
         name="load",
     )(*[pltpu.with_memory_space_constraint(a, pltpu.HBM) for a in arrays])
 
 
-def conv_kernel(me, xa, xb, ea, eb, w, first, second, mid, ext, cols):
+def conv_kernel(me, xa, xb, ea, eb, w, first, second, cols, ext):
     n, ch = xa.shape
     core = me[0] % 2
+    odd = me[1] % 2
     if ea.shape[0] == EDGE:
         edge_a, edge_b = ea[...], eb[...]
     else:
         edge_a = ea[pl.ds(pl.multiple_of(core * (n - EDGE), 16), EDGE), :]
         edge_b = eb[pl.ds(pl.multiple_of((1 - core) * (n - EDGE), 16), EDGE), :]
-    odd = me[1] % 2
     ext[pl.ds(pl.multiple_of(EDGE + core * n, 16), n), :] = xa[...]
     ext[pl.ds(pl.multiple_of(EDGE + (1 - core) * n, 16), n), :] = xb[...]
     far = EDGE + 2 * n
@@ -169,12 +177,12 @@
     ext[pl.ds(pl.multiple_of(core * far, 16), EDGE), :] = edge_b
     for b in range(3):
         cols[:, b * ch : (b + 1) * ch] = ext[EDGE - 1 + b : EDGE - 1 + b + 2 * n, :]
-    for a, out in ((2 * odd, first), (2 - 2 * odd, second), (1, mid)):
+    for a, out in ((odd, first), (1 - odd, second)):
         taps = w[pl.ds(pl.multiple_of(a * 3 * ch, 16), 3 * ch), :]
         out[...] = jnp.dot(cols[...], taps, preferred_element_type=F32).astype(out.dtype)
 
 
-def conv_half(me, xa, xb, ea, eb, w):
+def conv_sides(me, xa, xb, ea, eb, w):
     n, ch = xa.shape
     width = w.shape[1]
     return pl.pallas_call(
@@ -182,105 +190,131 @@
         out_shape=(
             vout((2 * n, width), BF16),
             vout((2 * n, width), BF16),
-            vout((2 * n, width), F32),
+            vout((2 * n, 3 * ch), BF16),
         ),
         in_specs=[sspec()] + [vspec()] * 5,
         out_specs=(vspec(),) * 3,
-        scratch_shapes=[
-            VMEM((2 * n + 2 * EDGE, ch), BF16),
-            VMEM((2 * n, 3 * ch), BF16),
-        ],
-        compiler_params=pltpu.CompilerParams(vmem_limit_bytes=12 << 20),
+        scratch_shapes=[VMEM((2 * n + 2 * EDGE, ch), BF16)],
+        compiler_params=pltpu.CompilerParams(vmem_limit_bytes=6 << 20),
         cost_estimate=pl.CostEstimate(
-            flops=2 * 2 * n * 9 * ch * width, bytes_accessed=2 * 9 * ch * width, transcendentals=0
-        ),
-        name="conv_half",
+            flops=2 * 2 * n * 6 * ch * width, bytes_accessed=2 * 6 * ch * width, transcendentals=0
+        ),
+        name="conv_sides",
     )(me, xa, xb, ea, eb, w)
 
 
-def residual_kernel(me, first, second, mid, xa, xb, *rest):
-    out = rest[-1]
-    n = xa.shape[0]
+def middle_kernel(me, cols, w, mid, own, valid):
+    lane = me[0]
+    ch = cols.shape[1] // 3
     width = mid.shape[1]
-    lane = me[0]
-    core = lane % 2
+    mid[...] = jnp.dot(cols[...], w[...], preferred_element_type=F32)
+    own[...] = cols[:, pl.ds(pl.multiple_of(ch + lane * width, width), width)].astype(F32)
     inner = jnp.logical_and(me[1] > 0, me[1] < me[2] - 1)
-    at = pl.ds(pl.multiple_of(lane * width, width), width)
-    for x, place in ((xa, core), (xb, 1 - core)):
-        rows = pl.ds(pl.multiple_of(place * n, 16), n)
-        south = second[rows, :].astype(F32)
-        south = jnp.where(inner, south, jnp.zeros_like(south))
-        conv_out = first[rows, :].astype(F32) + south + mid[rows, :]
-        out[rows, :] = (x[:, at].astype(F32) + conv_out.astype(BF16).astype(F32)).astype(BF16)
-    if len(rest) == 2:
-        out[2 * n : 2 * n + H, :] = rest[0][...]
-
-
-def residual_of(me, first, second, mid, xa, xb, *extra):
-    rows, width = mid.shape
-    rows += H * len(extra)
-    return pl.pallas_call(
-        residual_kernel,
-        out_shape=vout((rows, width), BF16),
-        in_specs=[sspec()] + [vspec()] * (5 + len(extra)),
-        out_specs=vspec(),
+    valid[...] = jnp.where(inner, jnp.ones(valid.shape, F32), jnp.zeros(valid.shape, F32))
+
+
+def conv_middle(me, cols, w):
+    rows, depth = cols.shape
+    width = w.shape[1]
+    return pl.pallas_call(
+        middle_kernel,
+        out_shape=(
+            vout((rows, width), F32),
+            vout((rows, width), F32),
+            vout((1, width), F32),
+        ),
+        in_specs=[sspec(), vspec(), vspec()],
+        out_specs=(vspec(),) * 3,
         compiler_params=pltpu.CompilerParams(vmem_limit_bytes=4 << 20),
         cost_estimate=pl.CostEstimate(
+            flops=2 * rows * depth * width, bytes_accessed=2 * depth * width, transcendentals=0
+        ),
+        name="conv_middle",
+    )(me, cols, w)
+
+
+def residual_of(first, second, mid, own, valid):
+    south = jnp.where(valid > 0.5, second.astype(F32), 0.0)
+    conv_out = (first.astype(F32) + south + mid).astype(BF16)
+    return (own + conv_out.astype(F32)).astype(BF16)
+
+
+def joined_kernel(first, second, mid, own, valid, bias, out):
+    rows = mid.shape[0]
+    out[0:rows, :] = residual_of(
+        first[...], second[...], mid[...], own[...], valid[...]
+    )
+    out[rows : rows + H, :] = bias[...]
+
+
+def joined_residual(first, second, mid, own, valid, bias):
+    rows, width = mid.shape
+    return pl.pallas_call(
+        joined_kernel,
+        out_shape=vout((rows + H, width), BF16),
+        in_specs=[vspec()] * 6,
+        out_specs=vspec(),
+        compiler_params=pltpu.CompilerParams(vmem_limit_bytes=2 << 20),
+        cost_estimate=pl.CostEstimate(
             flops=4 * rows * width, bytes_accessed=8 * rows * width, transcendentals=0
         ),
-        name="residual_of",
-    )(me, first, second, mid, xa, xb, *extra)
-
-
-def normed_of(blocks, gain, lane, ch, rows):
-    streams = [b[0:rows, :].astype(F32) for b in blocks]
-    square = sum(jnp.sum(s * s, axis=-1, keepdims=True) for s in streams)
-    factor = lax.rsqrt(square * (1.0 / ch) + 1e-06)
-    return [(s * factor * gain[lane ^ k]).astype(BF16) for k, s in enumerate(streams)]
-
-
-def keys_kernel(me, b0, b1, b2, b3, gain, w, k_out, v_out):
+        name="joined_residual",
+    )(first, second, mid, own, valid, bias)
+
+
+def factor_of(blocks, at, count, ch):
+    square = 0.0
+    for b in blocks:
+        stream = b[pl.ds(at, count), :].astype(F32)
+        square = square + jnp.sum(stream * stream, axis=-1, keepdims=True)
+    return lax.rsqrt(square * (1.0 / ch) + 1e-06)
+
+
+def keys_kernel(steps, me, b0, b1, b2, b3, gain, w, key_sum, value_sum, k_out, v_out):
     lane = me[0]
     rows, ch = k_out.shape
     width = b0.shape[1]
-    parts = normed_of((b0, b1, b2, b3), gain, lane, ch, rows)
-    for out, first in ((k_out, ch), (v_out, 2 * ch)):
-        acc = None
-        for k, part in enumerate(parts):
+    blocks = (b0, b1, b2, b3)
+    parts = [scaled(blocks[k], gain, lane, k, rows) for k in steps]
+    factor = factor_of(blocks, 0, rows, ch)
+    for out, acc, first in ((k_out, key_sum, ch), (v_out, value_sum, 2 * ch)):
+        total = acc[...]
+        for k, part in zip(steps, parts):
             at = pl.multiple_of((lane ^ k) * width, width)
-            term = jnp.dot(part, w[pl.ds(at, width), first : first + ch], preferred_element_type=F32)
-            acc = term if acc is None else acc + term
-        out[...] = acc.astype(BF16)
-
-
-def keys_of(me, blocks, gain, w):
+            total = total + jnp.dot(
+                part, w[pl.ds(at, width), first : first + ch], preferred_element_type=F32
+            )
+        out[...] = (total * factor).astype(BF16)
+
+
+def keys_of(me, steps, blocks, gain, w, sums):
     rows = blocks[0].shape[0]
     ch = w.shape[0]
     out = vout((rows, ch), BF16)
     return pl.pallas_call(
-        keys_kernel,
+        functools.partial(keys_kernel, steps),
         out_shape=(out, out),
-        in_specs=[sspec()] + [vspec()] * 6,
+        in_specs=[sspec()] + [vspec()] * 8,
         out_specs=(vspec(), vspec()),
-        compiler_params=pltpu.CompilerParams(vmem_limit_bytes=24 << 20),
+        compiler_params=pltpu.CompilerParams(vmem_limit_bytes=16 << 20),
         cost_estimate=pl.CostEstimate(
-            flops=2 * rows * ch * 2 * ch, bytes_accessed=4 * ch * ch, transcendentals=0
+            flops=2 * rows * ch * ch, bytes_accessed=2 * ch * ch, transcendentals=0
         ),
         name="keys_of",
-    )(me, *blocks, gain, w)
+    )(me, *blocks, gain, w, *sums)
 
 
 def scaled(block, gain, lane, k, rows):
     return (block[0:rows, :].astype(F32) * gain[lane ^ k]).astype(BF16)
 
 
-def project_kernel(steps, me, gain, w, *refs):
+def project_kernel(steps, count, me, gain, w, *refs):
     lane = me[0]
     blocks = refs[: len(steps)]
-    olds = refs[len(steps) : -3]
-    keys, values, query = refs[-3:]
-    rows, ch = keys.shape
-    n = query.shape[0]
+    olds = refs[len(steps) : -count]
+    outs = refs[-count:]
+    rows, ch = outs[0].shape
+    n = rows // 2
     width = blocks[0].shape[1]
     own = pl.multiple_of((lane % 2) * n, 16)
     parts = [scaled(b, gain, lane, k, rows) for b, k in zip(blocks, steps)]
@@ -288,9 +322,8 @@
         (b[pl.ds(own, n), :].astype(F32) * gain[lane ^ k]).astype(BF16)
         for b, k in zip(blocks, steps)
     ]
-    for i, (first, out, use) in enumerate(
-        ((ch, keys, parts), (2 * ch, values, parts), (0, query, owns))
-    ):
+    for i, out in enumerate(outs):
+        first, use = ((ch, parts), (2 * ch, parts), (0, owns))[i]
         acc = olds[i][...] if olds else None
         for k, part in zip(steps, use):
             at = pl.multiple_of((lane ^ k) * width, width)
@@ -299,14 +332,14 @@
         out[...] = acc
 
 
-def project(me, steps, blocks, gain, w, n, olds=()):
+def project(me, steps, blocks, gain, w, n, olds=(), count=3):
     rows = 2 * n
     ch, width = w.shape[0], blocks[0].shape[1]
     return pl.pallas_call(
-        functools.partial(project_kernel, steps),
-        out_shape=(vout((rows, ch), F32), vout((rows, ch), F32), vout((n, ch), F32)),
+        functools.partial(project_kernel, steps, count),
+        out_shape=(vout((rows, ch), F32), vout((rows, ch), F32), vout((n, ch), F32))[:count],
         in_specs=[sspec()] + [vspec()] * (2 + len(blocks) + len(olds)),
-        out_specs=(vspec(),) * 3,
+        out_specs=(vspec(),) * count,
         input_output_aliases={3 + len(blocks) + i: i for i in range(len(olds))},
         compiler_params=pltpu.CompilerParams(vmem_limit_bytes=16 << 20),
         cost_estimate=pl.CostEstimate(
@@ -331,13 +364,6 @@
     blocks = (b0, b1, b2, b3)
     own = pl.multiple_of(core * n, 16)
 
-    def factor_of(at, count):
-        square = 0.0
-        for b in blocks:
-            stream = b[pl.ds(at, count), :].astype(F32)
-            square = square + jnp.sum(stream * stream, axis=-1, keepdims=True)
-        return lax.rsqrt(square * (1.0 / ch) + 1e-06)
-
     for first, dst, acc, at, count in (
         (0, query, query_sum, own, n),
         (ch, keys, key_sum, 0, rows),
@@ -350,7 +376,7 @@
             total = total + jnp.dot(
                 part, w[pl.ds(place, width), first : first + ch], preferred_element_type=F32
             )
-        dst[0:count, :] = (total * factor_of(at, count)).astype(BF16)
+        dst[0:count, :] = (total * factor_of(blocks, at, count, ch)).astype(BF16)
     keys[rows : 2 * rows, :] = k_far[...]
     values[rows : 2 * rows, :] = v_far[...]
     pieces = []
@@ -369,15 +395,19 @@
         scores = lax.dot_general(
             stacked, keys[:, cols], (((1,), (1,)), ((), ())), preferred_element_type=F32
         )
-        values_g = values[:, cols]
-        result = jnp.zeros((n, 256), F32)
+        parts, totals = [], []
         for t in range(group):
             head = g * group + t
             s = scores[t * n : (t + 1) * n] + bias[head : head + 1, :]
             e = jnp.exp(s - jnp.max(s, axis=-1, keepdims=True))
-            total = jnp.sum(e, axis=-1, keepdims=True)
-            o = jnp.dot(e.astype(BF16), values_g, preferred_element_type=F32)
-            result = jnp.where(head_of == t, o / total, result)
+            totals.append(jnp.sum(e, axis=-1, keepdims=True))
+            parts.append(e.astype(BF16))
+        summed = jnp.dot(
+            jnp.concatenate(parts, axis=0), values[:, cols], preferred_element_type=F32
+        )
+        result = jnp.zeros((n, 256), F32)
+        for t in range(group):
+            result = jnp.where(head_of == t, summed[t * n : (t + 1) * n] / totals[t], result)
         attended[:, cols] = result.astype(BF16)
     for k, block in enumerate(blocks):
         at = pl.multiple_of((lane ^ k) * width, width)
@@ -444,24 +474,31 @@
     edge_d = swap(edge_y, 1)
     x_d = swap(x_y, 1)
     bias_own = jnp.pad(key_bias.reshape(n, H).T, ((0, 0), (0, width - n)))
-    x_v, conv_w = load(x, conv_weight)
-    near_parts = conv_half(me, x_v, x_c, edge_y, edge_d, conv_w)
-    za = lat_swap(near_parts[0], 0)
-    zb = lat_swap(near_parts[1], 1)
-    near = residual_of(me, za, zb, near_parts[2], x_v, x_c, bias_own)
+    taps = 3 * ch
+    x_v, side_w = load((x, conv_weight), (((0, n),), ((0, taps), (2 * taps, taps))))
+    za, zb, cols = conv_sides(me, x_v, x_c, edge_y, edge_d, side_w)
+    za = lat_swap(za, 0)
+    zb = lat_swap(zb, 1)
+    (mid_w,) = load((conv_weight,), (((taps, taps),),))
+    mid, own, valid = conv_middle(me, cols, mid_w)
+    near = joined_residual(za, zb, mid, own, valid, bias_own)
+    near_c = swap(near, 1)
     far_y = swap(near, 2)
-    near_c = swap(near, 1)
     far_d = swap(far_y, 1)
-    far_parts = conv_half(me, x_y, x_d, x_v, x_c, conv_w)
-    za = lat_swap(far_parts[0], 0)
-    zb = lat_swap(far_parts[1], 1)
-    far = residual_of(me, za, zb, far_parts[2], x_y, x_d)
+    za, zb, cols = conv_sides(me, x_y, x_d, x_v, x_c, side_w)
+    za = lat_swap(za, 0)
+    zb = lat_swap(zb, 1)
+    mid, own, valid = conv_middle(me, cols, mid_w)
+    far = residual_of(za, zb, mid, own, valid)
     near_y = swap(far, 2)
     far_c = swap(far, 1)
     near_d = swap(near_y, 1)
 
     gain = norm_gain.reshape(lon_size, 1, width)
-    k_far, v_far = keys_of(me, (far, far_c, far_y, far_d), gain, qkv_weight)
+    far_sums = project(me, (0, 1), (far, far_c), gain, qkv_weight, n, count=2)
+    k_far, v_far = keys_of(
+        me, (2, 3), (far, far_c, far_y, far_d), gain, qkv_weight, far_sums
+    )
     sums = project(me, (0, 1), (near, near_c), gain, qkv_weight, n)
     sums = project(me, (2,), (near_y,), gain, qkv_weight, n, sums)
     out = attend(

time: 53.7 us -> 54.9 us (1.022)
  Pallas kernels: 21.8 us -> 23.4 us
  starting transfers between devices: 13.8 us -> 13.2 us
    pallas_call x8 -> x11, Pallas kernels: 14.9 us -> 16.9 us  [the longest x3 4.82 us: project(): pl.pallas_call(functools.partial(project_kernel, steps, count), out_shape...]
    ppermute x4, waiting for transfers between devices: 2.49 us -> 0.62 us  [lat_swap(): return lax.ppermute(value, ('lon', 'lat'), pairs)]
    ppermute x11, waiting for transfers between devices: 14.4 us -> 16.2 us  [swap(): return lax.ppermute(value, 'lon', [(i, i ^ bit) for i in range(lon_size)])]
    ppermute x11, starting transfers between devices: 8.67 us -> 7.97 us  [swap(): return lax.ppermute(value, 'lon', [(i, i ^ bit) for i in range(lon_size)])]
  transfers between devices with their start and end apart: 15 -> 15, of which waited for: 5 -> 5; matrix products, arithmetic and copies ran while one was open for 2% -> 2% of each run, Pallas kernels for 28% -> 31%
where the time goes in v2:
time: 54.9 us; the launch traced here: 54.6 us
  Pallas kernels  23.4 us (43%)
  waiting for transfers between devices  16.8 us (31%)
  starting transfers between devices  13.2 us (24%)
  local copies, waits for them, and re-layouts  0.79 us (1%)
    ppermute x11, waiting for transfers between devices, swap(): return lax.ppermute(value, 'lon', [(i, i ^ bit) for i in range(lon_size)])  16.2 us
    ppermute x11, starting transfers between devices, swap(): return lax.ppermute(value, 'lon', [(i, i ^ bit) for i in range(lon_size)])  7.97 us
    pallas_call x1, Pallas kernels, attend(): pl.pallas_call(functools.partial(attend_kernel, steps), out_shape=jax.Sha...  6.55 us
    ppermute x4, starting transfers between devices, lat_swap(): return lax.ppermute(value, ('lon', 'lat'), pairs)  5.18 us
    pallas_call x3, Pallas kernels, project(): pl.pallas_call(functools.partial(project_kernel, steps, count), out_shape...  4.82 us
    pallas_call x2, Pallas kernels, conv_sides(): pl.pallas_call(conv_kernel, out_shape=(vout((2 * n, width), BF16), vout((...  4.1 us
    pallas_call x2, Pallas kernels, load(): pl.pallas_call(functools.partial(load_kernel, tuple(pieces)), out_shape=t...  3.64 us
    pallas_call x2, Pallas kernels, conv_middle(): pl.pallas_call(middle_kernel, out_shape=(vout((rows, width), F32), vout((...  2.62 us
  transfers between devices with their start and end apart: 15, of which 5 were waited for; matrix products, arithmetic and copies ran while one was open for 2% of the time, Pallas kernels for 31%

profile of v2, /device:TPU:0, one launch (start us, length us, event | category | flops | bytes accessed | tf_op | source)
XLA Modules:
  0.0 54.6 jit_solution(8577757875102260575)
XLA Ops:
  0.0 3.0 %collective-permute-start.6 = (bf16[192,1024]{1,0:T(8,128)(2,1)}, bf16[192,1024]{1,0:T(8,128)(2,1)S(1)}, u32[]{:S(2)}, u32[]{:S(2)}) collective-permute-start(bf16[192,1024]{1,0:T(8,128)(2,1)} %bitcast.17), channel_id=1, source_target_pairs={{0,8},{4,12},{8,0},{12,4},{1,9},{5,13},{9,1},{13,5},{2,10},{6,14},... | collective-permute-start | bytes 1179656 | tf_op jit(solution)/shard_map/ppermute | solution.py:454
  3.0 0.0 collective-permute-start
  3.0 9.3 %collective-permute-done.6.xa = bf16[192,1024]{1,0:T(8,128)(2,1)S(1)} collective-permute-done((bf16[192,1024]{1,0:T(8,128)(2,1)}, bf16[192,1024]{1,0:T(8,128)(2,1)S(1)}, u32[]{:S(2)}, u32[]{:S(2)}) %collective-permute-start.6) | collective-permute-done | bytes 393248 | tf_op jit(solution)/shard_map/ppermute | solution.py:454
  12.3 0.8 %dynamic-slice_bitcast_fusion = bf16[16,1024]{1,0:T(8,128)(2,1)S(1)} fusion(bf16[1,192,1024]{2,1,0:T(8,128)(2,1)} %param.6, s32[]{:T(128)S(6)} %select_n.15), kind=kLoop, calls=%fused_computation.2 | loop fusion | bytes 65540 | tf_op jit(solution)/shard_map/dynamic_slice | solution.py:470
  13.1 1.7 %collective-permute-start.1 = (bf16[16,1024]{1,0:T(8,128)(2,1)S(1)}, bf16[16,1024]{1,0:T(8,128)(2,1)S(1)}, u32[]{:S(2)}, u32[]{:S(2)}) collective-permute-start(bf16[16,1024]{1,0:T(8,128)(2,1)S(1)} %dynamic-slice_bitcast_fusion), channel_id=1, source_target_pairs={{0,8},{4,12},{8,0},{12,4},{1,9},{5,13},{9,1},{13,5},{2,10},{6,14},... | collective-permute-start | bytes 98312 | tf_op jit(solution)/shard_map/ppermute | solution.py:454
  14.8 2.2 %collective-permute-done.1.ea = bf16[16,1024]{1,0:T(8,128)(2,1)S(1)} collective-permute-done((bf16[16,1024]{1,0:T(8,128)(2,1)S(1)}, bf16[16,1024]{1,0:T(8,128)(2,1)S(1)}, u32[]{:S(2)}, u32[]{:S(2)}) %collective-permute-start.1) | collective-permute-done | bytes 32800 | tf_op jit(solution)/shard_map/ppermute | solution.py:454
  17.0 0.1 pad_add_fusion.me
  17.1 2.1 %load.2 = (bf16[192,1024]{1,0:T(8,128)(2,1)S(1)}, bf16[6144,256]{1,0:T(8,128)(2,1)S(1)}) custom-call(bf16[192,1024]{1,0:T(8,128)(2,1)} %bitcast.19, bf16[9216,256]{1,0:T(8,128)(2,1)} %refs_0_.1), custom_call_target="tpu_custom_call" | custom-call | bytes 3538944 | tf_op jit(solution)/shard_map/load/pallas_call | solution.py:152
  19.2 2.1 %conv_sides.2 = (bf16[384,256]{1,0:T(8,128)(2,1)S(1)}, bf16[384,256]{1,0:T(8,128)(2,1)S(1)}, bf16[384,3072]{1,0:T(8,128)(2,1)S(1)}) custom-call(s32[3]{0:T(128)S(1)} %pad_add_fusion.me, bf16[192,1024]{1,0:T(8,128)(2,1)S(1)} %get-tuple-element.29.xa.ea, bf16[192,1024]{1,0:T(8,128)(2,1)S(1)} %collective-permute-done.xb.eb, ...), custom_call_target="tpu_custom_call" | custom-call | flops 1207959552 | bytes 3145728 | tf_op jit(solution)/shard_map/conv_sides/pallas_call | solution.py:188
  21.3 1.9 %collective-permute-start.3 = (bf16[384,256]{1,0:T(8,128)(2,1)S(1)}, bf16[384,256]{1,0:T(8,128)(2,1)S(1)}, u32[]{:S(2)}, u32[]{:S(2)}) collective-permute-start(bf16[384,256]{1,0:T(8,128)(2,1)S(1)} %get-tuple-element.31), channel_id=1, source_target_pairs={{0,1},{1,0},{2,3},{3,2},{4,5},{5,4},{6,7},{7,6},{8,9},{9,8},{10,11... | collective-permute-start | bytes 589832 | tf_op jit(solution)/shard_map/ppermute | solution.py:467
  23.1 0.3 collective-permute-start.4
  23.4 1.5 %load.3.w = bf16[3072,256]{1,0:T(8,128)(2,1)S(1)} custom-call(bf16[9216,256]{1,0:T(8,128)(2,1)} %refs_0_.1), custom_call_target="tpu_custom_call" | custom-call | bytes 1572864 | tf_op jit(solution)/shard_map/load/pallas_call | solution.py:152
  25.0 0.0 slice-start
  25.0 2.1 %conv_sides.3 = (bf16[384,256]{1,0:T(8,128)(2,1)S(1)}, bf16[384,256]{1,0:T(8,128)(2,1)S(1)}, bf16[384,3072]{1,0:T(8,128)(2,1)S(1)}) custom-call(s32[3]{0:T(128)S(1)} %pad_add_fusion.me, bf16[192,1024]{1,0:T(8,128)(2,1)S(1)} %collective-permute-done.6.xa, bf16[192,1024]{1,0:T(8,128)(2,1)S(1)} %collective-permute-done.7.xb, ...), custom_call_target="tpu_custom_call" | custom-call | flops 1207959552 | bytes 3145728 | tf_op jit(solution)/shard_map/conv_sides/pallas_call | solution.py:188
  27.1 0.3 collective-permute-start.9
  27.4 2.7 %collective-permute-start.8 = (bf16[384,256]{1,0:T(8,128)(2,1)S(1)}, bf16[384,256]{1,0:T(8,128)(2,1)S(1)}, u32[]{:S(2)}, u32[]{:S(2)}) collective-permute-start(bf16[384,256]{1,0:T(8,128)(2,1)S(1)} %get-tuple-element.39), channel_id=1, source_target_pairs={{0,1},{1,0},{2,3},{3,2},{4,5},{5,4},{6,7},{7,6},{8,9},{9,8},{10,11... | collective-permute-start | bytes 589832 | tf_op jit(solution)/shard_map/ppermute | solution.py:467
  30.1 1.3 %conv_middle.2 = (f32[384,256]{1,0:T(8,128)S(1)}, f32[384,256]{1,0:T(8,128)S(1)}, f32[1,256]{1,0:T(1,128)S(1)}) custom-call(s32[3]{0:T(128)S(1)} %pad_add_fusion.me, bf16[384,3072]{1,0:T(8,128)(2,1)S(1)} %get-tuple-element.33.cols, bf16[3072,256]{1,0:T(8,128)(2,1)S(1)} %load.3.w), custom_call_target="tpu_custom_call" | custom-call | flops 603979776 | bytes 1572864 | tf_op jit(solution)/shard_map/conv_middle/pallas_call | solution.py:219
  31.4 0.1 joined_residual.1.refs_0_.b0
  31.6 0.1 collective-permute-start.5
  31.6 1.6 %collective-permute-start.13 = (bf16[400,256]{1,0:T(8,128)(2,1)S(1)}, bf16[400,256]{1,0:T(8,128)(2,1)S(1)}, u32[]{:S(2)}, u32[]{:S(2)}) collective-permute-start(bf16[400,256]{1,0:T(8,128)(2,1)S(1)} %joined_residual.1.refs_0_.b0), channel_id=1, source_target_pairs={{0,8},{4,12},{8,0},{12,4},{1,9},{5,13},{9,1},{13,5},{2,10},{6,14},... | collective-permute-start | bytes 614408 | tf_op jit(solution)/shard_map/ppermute | solution.py:454
  33.2 1.3 %conv_middle.3 = (f32[384,256]{1,0:T(8,128)S(1)}, f32[384,256]{1,0:T(8,128)S(1)}, f32[1,256]{1,0:T(1,128)S(1)}) custom-call(s32[3]{0:T(128)S(1)} %pad_add_fusion.me, bf16[384,3072]{1,0:T(8,128)(2,1)S(1)} %get-tuple-element.37.cols, bf16[3072,256]{1,0:T(8,128)(2,1)S(1)} %load.3.w), custom_call_target="tpu_custom_call" | custom-call | flops 603979776 | bytes 1572864 | tf_op jit(solution)/shard_map/conv_middle/pallas_call | solution.py:219
  34.6 0.6 %collective-permute-done.8 = bf16[384,256]{1,0:T(8,128)(2,1)S(1)} collective-permute-done((bf16[384,256]{1,0:T(8,128)(2,1)S(1)}, bf16[384,256]{1,0:T(8,128)(2,1)S(1)}, u32[]{:S(2)}, u32[]{:S(2)}) %collective-permute-start.8) | collective-permute-done | bytes 196640 | tf_op jit(solution)/shard_map/ppermute | solution.py:467
  35.2 0.1 add_convert_fusion.refs_0_.b0
  35.3 1.6 %collective-permute-start.10 = (bf16[384,256]{1,0:T(8,128)(2,1)S(1)}, bf16[384,256]{1,0:T(8,128)(2,1)S(1)}, u32[]{:S(2)}, u32[]{:S(2)}) collective-permute-start(bf16[384,256]{1,0:T(8,128)(2,1)S(1)} %add_convert_fusion.refs_0_.b0), channel_id=1, source_target_pairs={{0,8},{4,12},{8,0},{12,4},{1,9},{5,13},{9,1},{13,5},{2,10},{6,14},... | collective-permute-start | bytes 589832 | tf_op jit(solution)/shard_map/ppermute | solution.py:454
  36.8 2.8 %collective-permute-done.13.b2.bias_y = bf16[400,256]{1,0:T(8,128)(2,1)S(1)} collective-permute-done((bf16[400,256]{1,0:T(8,128)(2,1)S(1)}, bf16[400,256]{1,0:T(8,128)(2,1)S(1)}, u32[]{:S(2)}, u32[]{:S(2)}) %collective-permute-start.13) | collective-permute-done | bytes 204832 | tf_op jit(solution)/shard_map/ppermute | solution.py:454
  39.7 1.7 %project.3 = (f32[384,1024]{1,0:T(8,128)S(1)}, f32[384,1024]{1,0:T(8,128)S(1)}, f32[192,1024]{1,0:T(8,128)S(1)}) custom-call(s32[3]{0:T(128)S(1)} %pad_add_fusion.me, f32[4,1,256]{2,1,0:T(1,128)S(1)} %bitcast.12, bf16[1024,3072]{1,0:T(8,128)(2,1)S(1)} %bitcast.11, bf16[400,256]{1,0:T(8,128)(2,1)S(1)} %joined_residual.1.refs_0_.b0, ...), custom_call_target="tpu_custom_call" | custom-call | flops 1006632960 | bytes 3145728 | tf_op jit(solution)/shard_map/project/pallas_call | solution.py:338
  41.4 1.9 %collective-permute-done.10.refs_0_.b2 = bf16[384,256]{1,0:T(8,128)(2,1)S(1)} collective-permute-done((bf16[384,256]{1,0:T(8,128)(2,1)S(1)}, bf16[384,256]{1,0:T(8,128)(2,1)S(1)}, u32[]{:S(2)}, u32[]{:S(2)}) %collective-permute-start.10) | collective-permute-done | bytes 196640 | tf_op jit(solution)/shard_map/ppermute | solution.py:454
  43.3 1.6 %project.4 = (f32[384,1024]{1,0:T(8,128)S(1)}, f32[384,1024]{1,0:T(8,128)S(1)}, f32[192,1024]{1,0:T(8,128)S(1)}) custom-call(s32[3]{0:T(128)S(1)} %pad_add_fusion.me, f32[4,1,256]{2,1,0:T(1,128)S(1)} %bitcast.13, bf16[1024,3072]{1,0:T(8,128)(2,1)S(1)} %bitcast.11, ...), custom_call_target="tpu_custom_call", output_to_operand_aliasing={{0}: (4, {}), {1}: (5, {}), {2}: (6, {})} | custom-call | flops 503316480 | bytes 1572864 | tf_op jit(solution)/shard_map/project/pallas_call | solution.py:338
  44.9 1.5 %project.5 = (f32[384,1024]{1,0:T(8,128)S(1)}, f32[384,1024]{1,0:T(8,128)S(1)}) custom-call(s32[3]{0:T(128)S(1)} %pad_add_fusion.me, f32[4,1,256]{2,1,0:T(1,128)S(1)} %bitcast.14, bf16[1024,3072]{1,0:T(8,128)(2,1)S(1)} %bitcast.11, bf16[384,256]{1,0:T(8,128)(2,1)S(1)} %add_convert_fusion.refs_0_.b0, bf16[384,256]{1,0:T(8,128)(2,1)S(1)} %collective-permute-done.12.refs_1_.b1), custom_call_target="tpu_custom_call" | custom-call | flops 1006632960 | bytes 3145728 | tf_op jit(solution)/shard_map/project/pallas_call | solution.py:338
  46.5 0.0 copy-start
  46.5 1.6 %keys_of.1 = (bf16[384,1024]{1,0:T(8,128)(2,1)S(1)}, bf16[384,1024]{1,0:T(8,128)(2,1)S(1)}) custom-call(s32[3]{0:T(128)S(1)} %pad_add_fusion.me, bf16[384,256]{1,0:T(8,128)(2,1)S(1)} %add_convert_fusion.refs_0_.b0, bf16[384,256]{1,0:T(8,128)(2,1)S(1)} %collective-permute-done.12.refs_1_.b1, bf16[400,256]{1,0:T(8,128)(2,1)S(1)} %collective-permute-done.13.b2.bias_y, ...), custom_call_target="tpu_custom_call" | custom-call | flops 805306368 | bytes 2097152 | tf_op jit(solution)/shard_map/keys_of/pallas_call | solution.py:294
  48.1 6.5 %attend.1 = bf16[192,1024]{1,0:T(8,128)(2,1)} custom-call(s32[3]{0:T(128)S(1)} %pad_add_fusion.me, bf16[400,256]{1,0:T(8,128)(2,1)S(1)} %joined_residual.1.refs_0_.b0, bf16[400,256]{1,0:T(8,128)(2,1)S(1)} %collective-permute-done.5.refs_1_.b1, bf16[384,256]{1,0:T(8,128)(2,1)S(1)} %collective-permute-done.10.refs_0_.b2, ...), custom_call_target="tpu_custom_call" | custom-call | flops 3221225472 | bytes 8388608 | tf_op jit(solution)/shard_map/attend/pallas_call | solution.py:423
  (26 shorter events, 0.1 us)
Async XLA Ops:
  0.0 12.3 %collective-permute-start.6 = (bf16[192,1024]{1,0:T(8,128)(2,1)}, bf16[192,1024]{1,0:T(8,128)(2,1)S(1)}, u32[]{:S(2)}, u32[]{:S(2)}) collective-permute-start(bf16[192,1024]{1,0:T(8,128)(2,1)} %bitcast.17), channel_id=1, source_target_pairs={{0,8},{4,12},{8,0},{12,4},{1,9},{5,13},{9,1},{13,5},{2,10},{6,14},... | collective-permute-start | bytes 1179656 | tf_op jit(solution)/shard_map/ppermute | solution.py:454
  3.0 16.2 %collective-permute-start = (bf16[192,1024]{1,0:T(8,128)(2,1)}, bf16[192,1024]{1,0:T(8,128)(2,1)S(1)}, u32[]{:S(2)}, u32[]{:S(2)}) collective-permute-start(bf16[192,1024]{1,0:T(8,128)(2,1)} %bitcast.18), channel_id=1, source_target_pairs={{0,4},{4,0},{8,12},{12,8},{1,5},{5,1},{9,13},{13,9},{2,6},{6,2},{1... | collective-permute-start | bytes 1179656 | tf_op jit(solution)/shard_map/ppermute | solution.py:454
  12.3 12.7 %collective-permute-start.7 = (bf16[192,1024]{1,0:T(8,128)(2,1)S(1)}, bf16[192,1024]{1,0:T(8,128)(2,1)S(1)}, u32[]{:S(2)}, u32[]{:S(2)}) collective-permute-start(bf16[192,1024]{1,0:T(8,128)(2,1)S(1)} %collective-permute-done.6.xa), channel_id=1, source_target_pairs={{0,4},{4,0},{8,12},{12,8},{1,5},{5,1},{9,13},{13,9},{2,6},{6,2},{1... | collective-permute-start | bytes 1179656 | tf_op jit(solution)/shard_map/ppermute | solution.py:454
  13.1 3.9 %collective-permute-start.1 = (bf16[16,1024]{1,0:T(8,128)(2,1)S(1)}, bf16[16,1024]{1,0:T(8,128)(2,1)S(1)}, u32[]{:S(2)}, u32[]{:S(2)}) collective-permute-start(bf16[16,1024]{1,0:T(8,128)(2,1)S(1)} %dynamic-slice_bitcast_fusion), channel_id=1, source_target_pairs={{0,8},{4,12},{8,0},{12,4},{1,9},{5,13},{9,1},{13,5},{2,10},{6,14},... | collective-permute-start | bytes 98312 | tf_op jit(solution)/shard_map/ppermute | solution.py:454
  17.0 2.2 %collective-permute-start.2 = (bf16[16,1024]{1,0:T(8,128)(2,1)S(1)}, bf16[16,1024]{1,0:T(8,128)(2,1)S(1)}, u32[]{:S(2)}, u32[]{:S(2)}) collective-permute-start(bf16[16,1024]{1,0:T(8,128)(2,1)S(1)} %collective-permute-done.1.ea), channel_id=1, source_target_pairs={{0,4},{4,0},{8,12},{12,8},{1,5},{5,1},{9,13},{13,9},{2,6},{6,2},{1... | collective-permute-start | bytes 98312 | tf_op jit(solution)/shard_map/ppermute | solution.py:454
  21.3 10.1 %collective-permute-start.3 = (bf16[384,256]{1,0:T(8,128)(2,1)S(1)}, bf16[384,256]{1,0:T(8,128)(2,1)S(1)}, u32[]{:S(2)}, u32[]{:S(2)}) collective-permute-start(bf16[384,256]{1,0:T(8,128)(2,1)S(1)} %get-tuple-element.31), channel_id=1, source_target_pairs={{0,1},{1,0},{2,3},{3,2},{4,5},{5,4},{6,7},{7,6},{8,9},{9,8},{10,11... | collective-permute-start | bytes 589832 | tf_op jit(solution)/shard_map/ppermute | solution.py:467
  23.1 1.8 %copy-start.2 = (bf16[1,192,16]{1,2,0:T(8,128)(2,1)S(1)}, bf16[1,192,16]{1,2,0:T(8,128)(2,1)}, u32[]{:S(2)}) copy-start(bf16[1,192,16]{1,2,0:T(8,128)(2,1)} %param.11) | copy-start | bytes 18436
  23.1 8.3 %collective-permute-start.4 = (bf16[384,256]{1,0:T(8,128)(2,1)S(1)}, bf16[384,256]{1,0:T(8,128)(2,1)S(1)}, u32[]{:S(2)}, u32[]{:S(2)}) collective-permute-start(bf16[384,256]{1,0:T(8,128)(2,1)S(1)} %get-tuple-element.32), channel_id=1, source_target_pairs={{0,4},{1,2},{2,1},{3,7},{4,0},{5,6},{6,5},{7,3},{8,12},{9,10},{10,... | collective-permute-start | bytes 589832 | tf_op jit(solution)/shard_map/ppermute | solution.py:467
  25.0 14.7 %slice-start = ((s8[6291456]{0:T(1024)(128)(4,1)}), s8[4194304]{0:T(1024)(128)(4,1)S(1)}, s32[]{:S(2)}) async-start(s8[6291456]{0:T(1024)(128)(4,1)} %bitcast.10), calls=%async_computation | async-start | bytes 8388608
  27.1 7.5 %collective-permute-start.9 = (bf16[384,256]{1,0:T(8,128)(2,1)S(1)}, bf16[384,256]{1,0:T(8,128)(2,1)S(1)}, u32[]{:S(2)}, u32[]{:S(2)}) collective-permute-start(bf16[384,256]{1,0:T(8,128)(2,1)S(1)} %get-tuple-element.41), channel_id=1, source_target_pairs={{0,4},{1,2},{2,1},{3,7},{4,0},{5,6},{6,5},{7,3},{8,12},{9,10},{10,... | collective-permute-start | bytes 589832 | tf_op jit(solution)/shard_map/ppermute | solution.py:467
  27.4 7.8 %collective-permute-start.8 = (bf16[384,256]{1,0:T(8,128)(2,1)S(1)}, bf16[384,256]{1,0:T(8,128)(2,1)S(1)}, u32[]{:S(2)}, u32[]{:S(2)}) collective-permute-start(bf16[384,256]{1,0:T(8,128)(2,1)S(1)} %get-tuple-element.39), channel_id=1, source_target_pairs={{0,1},{1,0},{2,3},{3,2},{4,5},{5,4},{6,7},{7,6},{8,9},{9,8},{10,11... | collective-permute-start | bytes 589832 | tf_op jit(solution)/shard_map/ppermute | solution.py:467
  30.1 9.6 %slice-start.1 = ((s8[6291456]{0:T(1024)(128)(4,1)}), s8[2097152]{0:T(1024)(128)(4,1)S(1)}, s32[]{:S(2)}) async-start(s8[6291456]{0:T(1024)(128)(4,1)} %bitcast.10), calls=%async_computation.1 | async-start | bytes 4194304
  31.6 8.1 %collective-permute-start.5 = (bf16[400,256]{1,0:T(8,128)(2,1)S(1)}, bf16[400,256]{1,0:T(8,128)(2,1)S(1)}, u32[]{:S(2)}, u32[]{:S(2)}) collective-permute-start(bf16[400,256]{1,0:T(8,128)(2,1)S(1)} %joined_residual.1.refs_0_.b0), channel_id=1, source_target_pairs={{0,4},{4,0},{8,12},{12,8},{1,5},{5,1},{9,13},{13,9},{2,6},{6,2},{1... | collective-permute-start | bytes 614408 | tf_op jit(solution)/shard_map/ppermute | solution.py:454
  31.6 8.0 %collective-permute-start.13 = (bf16[400,256]{1,0:T(8,128)(2,1)S(1)}, bf16[400,256]{1,0:T(8,128)(2,1)S(1)}, u32[]{:S(2)}, u32[]{:S(2)}) collective-permute-start(bf16[400,256]{1,0:T(8,128)(2,1)S(1)} %joined_residual.1.refs_0_.b0), channel_id=1, source_target_pairs={{0,8},{4,12},{8,0},{12,4},{1,9},{5,13},{9,1},{13,5},{2,10},{6,14},... | collective-permute-start | bytes 614408 | tf_op jit(solution)/shard_map/ppermute | solution.py:454
  33.2 6.5 %copy-start.1 = (f32[1024]{0:T(1024)S(1)}, f32[1024]{0:T(1024)}, u32[]{:S(2)}) copy-start(f32[1024]{0:T(1024)} %param.8) | copy-start | bytes 12292
  35.3 8.1 %collective-permute-start.10 = (bf16[384,256]{1,0:T(8,128)(2,1)S(1)}, bf16[384,256]{1,0:T(8,128)(2,1)S(1)}, u32[]{:S(2)}, u32[]{:S(2)}) collective-permute-start(bf16[384,256]{1,0:T(8,128)(2,1)S(1)} %add_convert_fusion.refs_0_.b0), channel_id=1, source_target_pairs={{0,8},{4,12},{8,0},{12,4},{1,9},{5,13},{9,1},{13,5},{2,10},{6,14},... | collective-permute-start | bytes 589832 | tf_op jit(solution)/shard_map/ppermute | solution.py:454
  36.8 8.1 %collective-permute-start.12 = (bf16[384,256]{1,0:T(8,128)(2,1)S(1)}, bf16[384,256]{1,0:T(8,128)(2,1)S(1)}, u32[]{:S(2)}, u32[]{:S(2)}) collective-permute-start(bf16[384,256]{1,0:T(8,128)(2,1)S(1)} %add_convert_fusion.refs_0_.b0), channel_id=1, source_target_pairs={{0,4},{4,0},{8,12},{12,8},{1,5},{5,1},{9,13},{13,9},{2,6},{6,2},{1... | collective-permute-start | bytes 589832 | tf_op jit(solution)/shard_map/ppermute | solution.py:454
  39.7 6.8 %collective-permute-start.14 = (bf16[400,256]{1,0:T(8,128)(2,1)S(1)}, bf16[400,256]{1,0:T(8,128)(2,1)S(1)}, u32[]{:S(2)}, u32[]{:S(2)}) collective-permute-start(bf16[400,256]{1,0:T(8,128)(2,1)S(1)} %collective-permute-done.13.b2.bias_y), channel_id=1, source_target_pairs={{0,4},{4,0},{8,12},{12,8},{1,5},{5,1},{9,13},{13,9},{2,6},{6,2},{1... | collective-permute-start | bytes 614408 | tf_op jit(solution)/shard_map/ppermute | solution.py:454
  43.3 4.7 %collective-permute-start.11 = (bf16[384,256]{1,0:T(8,128)(2,1)S(1)}, bf16[384,256]{1,0:T(8,128)(2,1)S(1)}, u32[]{:S(2)}, u32[]{:S(2)}) collective-permute-start(bf16[384,256]{1,0:T(8,128)(2,1)S(1)} %collective-permute-done.10.refs_0_.b2), channel_id=1, source_target_pairs={{0,4},{4,0},{8,12},{12,8},{1,5},{5,1},{9,13},{13,9},{2,6},{6,2},{1... | collective-permute-start | bytes 589832 | tf_op jit(solution)/shard_map/ppermute | solution.py:454
  46.5 1.6 %copy-start = (bf16[1024,1024]{1,0:T(8,128)(2,1)S(1)}, bf16[1024,1024]{1,0:T(8,128)(2,1)}, u32[]{:S(2)}) copy-start(bf16[1024,1024]{1,0:T(8,128)(2,1)} %w_out.1) | copy-start | bytes 6291460

commit v3 on v2

--- a/solution.py
+++ b/solution.py
@@ -175,7 +175,9 @@
     far = EDGE + 2 * n
     ext[pl.ds(pl.multiple_of((1 - core) * far, 16), EDGE), :] = edge_a
     ext[pl.ds(pl.multiple_of(core * far, 16), EDGE), :] = edge_b
-    for b in range(3):
+    cols[pl.ds(pl.multiple_of(core * n, 16), n), ch : 2 * ch] = xa[...]
+    cols[pl.ds(pl.multiple_of((1 - core) * n, 16), n), ch : 2 * ch] = xb[...]
+    for b in (0, 2):
         cols[:, b * ch : (b + 1) * ch] = ext[EDGE - 1 + b : EDGE - 1 + b + 2 * n, :]
     for a, out in ((odd, first), (1 - odd, second)):
         taps = w[pl.ds(pl.multiple_of(a * 3 * ch, 16), 3 * ch), :]
@@ -329,18 +331,20 @@
             at = pl.multiple_of((lane ^ k) * width, width)
             term = jnp.dot(part, w[pl.ds(at, width), first : first + ch], preferred_element_type=F32)
             acc = term if acc is None else acc + term
-        out[...] = acc
-
-
-def project(me, steps, blocks, gain, w, n, olds=(), count=3):
+        out[...] = acc.astype(out.dtype)
+
+
+def project(me, steps, blocks, gain, w, n, olds=(), count=3, dtype=F32):
     rows = 2 * n
     ch, width = w.shape[0], blocks[0].shape[1]
     return pl.pallas_call(
         functools.partial(project_kernel, steps, count),
-        out_shape=(vout((rows, ch), F32), vout((rows, ch), F32), vout((n, ch), F32))[:count],
+        out_shape=(vout((rows, ch), dtype), vout((rows, ch), dtype), vout((n, ch), dtype))[:count],
         in_specs=[sspec()] + [vspec()] * (2 + len(blocks) + len(olds)),
         out_specs=(vspec(),) * count,
-        input_output_aliases={3 + len(blocks) + i: i for i in range(len(olds))},
+        input_output_aliases={
+            3 + len(blocks) + i: i for i, old in enumerate(olds) if old.dtype == dtype
+        },
         compiler_params=pltpu.CompilerParams(vmem_limit_bytes=16 << 20),
         cost_estimate=pl.CostEstimate(
             flops=2 * (2 * rows + n) * width * len(blocks) * ch,
@@ -369,7 +373,7 @@
         (ch, keys, key_sum, 0, rows),
         (2 * ch, values, value_sum, 0, rows),
     ):
-        total = acc[...]
+        total = acc[...].astype(F32)
         for k in steps:
             part = (blocks[k][pl.ds(at, count), :].astype(F32) * gain[lane ^ k]).astype(BF16)
             place = pl.multiple_of((lane ^ k) * width, width)
@@ -475,11 +479,13 @@
     x_d = swap(x_y, 1)
     bias_own = jnp.pad(key_bias.reshape(n, H).T, ((0, 0), (0, width - n)))
     taps = 3 * ch
-    x_v, side_w = load((x, conv_weight), (((0, n),), ((0, taps), (2 * taps, taps))))
+    x_v, side_w, mid_w = load(
+        (x, conv_weight, conv_weight),
+        (((0, n),), ((0, taps), (2 * taps, taps)), ((taps, taps),)),
+    )
     za, zb, cols = conv_sides(me, x_v, x_c, edge_y, edge_d, side_w)
     za = lat_swap(za, 0)
     zb = lat_swap(zb, 1)
-    (mid_w,) = load((conv_weight,), (((taps, taps),),))
     mid, own, valid = conv_middle(me, cols, mid_w)
     near = joined_residual(za, zb, mid, own, valid, bias_own)
     near_c = swap(near, 1)
@@ -500,7 +506,7 @@
         me, (2, 3), (far, far_c, far_y, far_d), gain, qkv_weight, far_sums
     )
     sums = project(me, (0, 1), (near, near_c), gain, qkv_weight, n)
-    sums = project(me, (2,), (near_y,), gain, qkv_weight, n, sums)
+    sums = project(me, (2,), (near_y,), gain, qkv_weight, n, sums, dtype=BF16)
     out = attend(
         me, (3,), (near, near_c, near_y, near_d), gain, qkv_weight, sums, k_far, v_far, far_y,
         far_d, out_weight

time: 54.9 us -> 53.7 us (0.978)
  Pallas kernels: 23.4 us -> 22.1 us
    pallas_call x2 -> x1, Pallas kernels: 3.64 us -> 2.66 us  [load(): pl.pallas_call(functools.partial(load_kernel, tuple(pieces)), out_shape=t...]
  transfers between devices with their start and end apart: 15 -> 15, of which waited for: 5 -> 5; matrix products, arithmetic and copies ran while one was open for 2% -> 2% of each run, Pallas kernels for 31% -> 29%
where the time goes in v3:
time: 53.7 us; the launch traced here: 53.3 us
  Pallas kernels  22.1 us (41%)
  waiting for transfers between devices  16.8 us (31%)
  starting transfers between devices  13.2 us (25%)
  local copies, waits for them, and re-layouts  0.79 us (1%)
    ppermute x11, waiting for transfers between devices, swap(): return lax.ppermute(value, 'lon', [(i, i ^ bit) for i in range(lon_size)])  16.2 us
    ppermute x11, starting transfers between devices, swap(): return lax.ppermute(value, 'lon', [(i, i ^ bit) for i in range(lon_size)])  7.99 us
    pallas_call x1, Pallas kernels, attend(): pl.pallas_call(functools.partial(attend_kernel, steps), out_shape=jax.Sha...  6.5 us
    ppermute x4, starting transfers between devices, lat_swap(): return lax.ppermute(value, ('lon', 'lat'), pairs)  5.16 us
    pallas_call x3, Pallas kernels, project(): pl.pallas_call(functools.partial(project_kernel, steps, count), out_shape...  4.49 us
    pallas_call x2, Pallas kernels, conv_sides(): pl.pallas_call(conv_kernel, out_shape=(vout((2 * n, width), BF16), vout((...  4.15 us
    pallas_call x1, Pallas kernels, load(): pl.pallas_call(functools.partial(load_kernel, tuple(pieces)), out_shape=t...  2.66 us
    pallas_call x2, Pallas kernels, conv_middle(): pl.pallas_call(middle_kernel, out_shape=(vout((rows, width), F32), vout((...  2.62 us
  transfers between devices with their start and end apart: 15, of which 5 were waited for; matrix products, arithmetic and copies ran while one was open for 2% of the time, Pallas kernels for 29%

profile of v3, /device:TPU:0, one launch (start us, length us, event | category | flops | bytes accessed | tf_op | source)
XLA Modules:
  0.0 53.3 jit_solution(13835161763933652562)
XLA Ops:
  0.0 3.0 %collective-permute-start.6 = (bf16[192,1024]{1,0:T(8,128)(2,1)}, bf16[192,1024]{1,0:T(8,128)(2,1)S(1)}, u32[]{:S(2)}, u32[]{:S(2)}) collective-permute-start(bf16[192,1024]{1,0:T(8,128)(2,1)} %bitcast.17), channel_id=1, source_target_pairs={{0,8},{4,12},{8,0},{12,4},{1,9},{5,13},{9,1},{13,5},{2,10},{6,14},... | collective-permute-start | bytes 1179656 | tf_op jit(solution)/shard_map/ppermute | solution.py:458
  3.0 0.0 collective-permute-start
  3.0 9.3 %collective-permute-done.6.xa = bf16[192,1024]{1,0:T(8,128)(2,1)S(1)} collective-permute-done((bf16[192,1024]{1,0:T(8,128)(2,1)}, bf16[192,1024]{1,0:T(8,128)(2,1)S(1)}, u32[]{:S(2)}, u32[]{:S(2)}) %collective-permute-start.6) | collective-permute-done | bytes 393248 | tf_op jit(solution)/shard_map/ppermute | solution.py:458
  12.3 0.8 %dynamic-slice_bitcast_fusion = bf16[16,1024]{1,0:T(8,128)(2,1)S(1)} fusion(bf16[1,192,1024]{2,1,0:T(8,128)(2,1)} %param.6, s32[]{:T(128)S(6)} %select_n.15), kind=kLoop, calls=%fused_computation.2 | loop fusion | bytes 65540 | tf_op jit(solution)/shard_map/dynamic_slice | solution.py:474
  13.1 1.7 %collective-permute-start.1 = (bf16[16,1024]{1,0:T(8,128)(2,1)S(1)}, bf16[16,1024]{1,0:T(8,128)(2,1)S(1)}, u32[]{:S(2)}, u32[]{:S(2)}) collective-permute-start(bf16[16,1024]{1,0:T(8,128)(2,1)S(1)} %dynamic-slice_bitcast_fusion), channel_id=1, source_target_pairs={{0,8},{4,12},{8,0},{12,4},{1,9},{5,13},{9,1},{13,5},{2,10},{6,14},... | collective-permute-start | bytes 98312 | tf_op jit(solution)/shard_map/ppermute | solution.py:458
  14.8 2.2 %collective-permute-done.1.ea = bf16[16,1024]{1,0:T(8,128)(2,1)S(1)} collective-permute-done((bf16[16,1024]{1,0:T(8,128)(2,1)S(1)}, bf16[16,1024]{1,0:T(8,128)(2,1)S(1)}, u32[]{:S(2)}, u32[]{:S(2)}) %collective-permute-start.1) | collective-permute-done | bytes 32800 | tf_op jit(solution)/shard_map/ppermute | solution.py:458
  17.0 0.1 pad_add_fusion.me
  17.1 2.7 %load.1 = (bf16[192,1024]{1,0:T(8,128)(2,1)S(1)}, bf16[6144,256]{1,0:T(8,128)(2,1)S(1)}, bf16[3072,256]{1,0:T(8,128)(2,1)S(1)}) custom-call(bf16[192,1024]{1,0:T(8,128)(2,1)} %bitcast.19, bf16[9216,256]{1,0:T(8,128)(2,1)} %refs_2_.1, bf16[9216,256]{1,0:T(8,128)(2,1)} %refs_2_.1), custom_call_target="tpu_custom_call" | custom-call | bytes 5111808 | tf_op jit(solution)/shard_map/load/pallas_call | solution.py:152
  19.8 0.0 copy-start.2
  19.8 2.1 %conv_sides.2 = (bf16[384,256]{1,0:T(8,128)(2,1)S(1)}, bf16[384,256]{1,0:T(8,128)(2,1)S(1)}, bf16[384,3072]{1,0:T(8,128)(2,1)S(1)}) custom-call(s32[3]{0:T(128)S(1)} %pad_add_fusion.me, bf16[192,1024]{1,0:T(8,128)(2,1)S(1)} %get-tuple-element.30.xa.ea, bf16[192,1024]{1,0:T(8,128)(2,1)S(1)} %collective-permute-done.xb.eb, ...), custom_call_target="tpu_custom_call" | custom-call | flops 1207959552 | bytes 3145728 | tf_op jit(solution)/shard_map/conv_sides/pallas_call | solution.py:190
  21.9 1.9 %collective-permute-start.3 = (bf16[384,256]{1,0:T(8,128)(2,1)S(1)}, bf16[384,256]{1,0:T(8,128)(2,1)S(1)}, u32[]{:S(2)}, u32[]{:S(2)}) collective-permute-start(bf16[384,256]{1,0:T(8,128)(2,1)S(1)} %get-tuple-element.32), channel_id=1, source_target_pairs={{0,1},{1,0},{2,3},{3,2},{4,5},{5,4},{6,7},{7,6},{8,9},{9,8},{10,11... | collective-permute-start | bytes 589832 | tf_op jit(solution)/shard_map/ppermute | solution.py:471
  23.7 0.3 collective-permute-start.4
  24.0 0.0 slice-start
  24.0 2.1 %conv_sides.3 = (bf16[384,256]{1,0:T(8,128)(2,1)S(1)}, bf16[384,256]{1,0:T(8,128)(2,1)S(1)}, bf16[384,3072]{1,0:T(8,128)(2,1)S(1)}) custom-call(s32[3]{0:T(128)S(1)} %pad_add_fusion.me, bf16[192,1024]{1,0:T(8,128)(2,1)S(1)} %collective-permute-done.6.xa, bf16[192,1024]{1,0:T(8,128)(2,1)S(1)} %collective-permute-done.7.xb, ...), custom_call_target="tpu_custom_call" | custom-call | flops 1207959552 | bytes 3145728 | tf_op jit(solution)/shard_map/conv_sides/pallas_call | solution.py:190
  26.1 0.3 collective-permute-start.9
  26.4 2.7 %collective-permute-start.8 = (bf16[384,256]{1,0:T(8,128)(2,1)S(1)}, bf16[384,256]{1,0:T(8,128)(2,1)S(1)}, u32[]{:S(2)}, u32[]{:S(2)}) collective-permute-start(bf16[384,256]{1,0:T(8,128)(2,1)S(1)} %get-tuple-element.41), channel_id=1, source_target_pairs={{0,1},{1,0},{2,3},{3,2},{4,5},{5,4},{6,7},{7,6},{8,9},{9,8},{10,11... | collective-permute-start | bytes 589832 | tf_op jit(solution)/shard_map/ppermute | solution.py:471
  29.1 1.3 %conv_middle.2 = (f32[384,256]{1,0:T(8,128)S(1)}, f32[384,256]{1,0:T(8,128)S(1)}, f32[1,256]{1,0:T(1,128)S(1)}) custom-call(s32[3]{0:T(128)S(1)} %pad_add_fusion.me, bf16[384,3072]{1,0:T(8,128)(2,1)S(1)} %get-tuple-element.34.cols, bf16[3072,256]{1,0:T(8,128)(2,1)S(1)} %get-tuple-element.35.w), custom_call_target="tpu_custom_call" | custom-call | flops 603979776 | bytes 1572864 | tf_op jit(solution)/shard_map/conv_middle/pallas_call | solution.py:221
  30.5 0.1 joined_residual.1.refs_0_.b0
  30.6 0.1 collective-permute-start.5
  30.7 1.6 %collective-permute-start.13 = (bf16[400,256]{1,0:T(8,128)(2,1)S(1)}, bf16[400,256]{1,0:T(8,128)(2,1)S(1)}, u32[]{:S(2)}, u32[]{:S(2)}) collective-permute-start(bf16[400,256]{1,0:T(8,128)(2,1)S(1)} %joined_residual.1.refs_0_.b0), channel_id=1, source_target_pairs={{0,8},{4,12},{8,0},{12,4},{1,9},{5,13},{9,1},{13,5},{2,10},{6,14},... | collective-permute-start | bytes 614408 | tf_op jit(solution)/shard_map/ppermute | solution.py:458
  32.3 1.3 %conv_middle.3 = (f32[384,256]{1,0:T(8,128)S(1)}, f32[384,256]{1,0:T(8,128)S(1)}, f32[1,256]{1,0:T(1,128)S(1)}) custom-call(s32[3]{0:T(128)S(1)} %pad_add_fusion.me, bf16[384,3072]{1,0:T(8,128)(2,1)S(1)} %get-tuple-element.39.cols, bf16[3072,256]{1,0:T(8,128)(2,1)S(1)} %get-tuple-element.35.w), custom_call_target="tpu_custom_call" | custom-call | flops 603979776 | bytes 1572864 | tf_op jit(solution)/shard_map/conv_middle/pallas_call | solution.py:221
  33.6 0.6 %collective-permute-done.8 = bf16[384,256]{1,0:T(8,128)(2,1)S(1)} collective-permute-done((bf16[384,256]{1,0:T(8,128)(2,1)S(1)}, bf16[384,256]{1,0:T(8,128)(2,1)S(1)}, u32[]{:S(2)}, u32[]{:S(2)}) %collective-permute-start.8) | collective-permute-done | bytes 196640 | tf_op jit(solution)/shard_map/ppermute | solution.py:471
  34.2 0.1 add_convert_fusion.refs_0_.b0
  34.3 1.6 %collective-permute-start.10 = (bf16[384,256]{1,0:T(8,128)(2,1)S(1)}, bf16[384,256]{1,0:T(8,128)(2,1)S(1)}, u32[]{:S(2)}, u32[]{:S(2)}) collective-permute-start(bf16[384,256]{1,0:T(8,128)(2,1)S(1)} %add_convert_fusion.refs_0_.b0), channel_id=1, source_target_pairs={{0,8},{4,12},{8,0},{12,4},{1,9},{5,13},{9,1},{13,5},{2,10},{6,14},... | collective-permute-start | bytes 589832 | tf_op jit(solution)/shard_map/ppermute | solution.py:458
  35.9 2.8 %collective-permute-done.13.b2.bias_y = bf16[400,256]{1,0:T(8,128)(2,1)S(1)} collective-permute-done((bf16[400,256]{1,0:T(8,128)(2,1)S(1)}, bf16[400,256]{1,0:T(8,128)(2,1)S(1)}, u32[]{:S(2)}, u32[]{:S(2)}) %collective-permute-start.13) | collective-permute-done | bytes 204832 | tf_op jit(solution)/shard_map/ppermute | solution.py:458
  38.7 1.7 %project.3 = (f32[384,1024]{1,0:T(8,128)S(1)}, f32[384,1024]{1,0:T(8,128)S(1)}, f32[192,1024]{1,0:T(8,128)S(1)}) custom-call(s32[3]{0:T(128)S(1)} %pad_add_fusion.me, f32[4,1,256]{2,1,0:T(1,128)S(1)} %bitcast.12, bf16[1024,3072]{1,0:T(8,128)(2,1)S(1)} %bitcast.11, bf16[400,256]{1,0:T(8,128)(2,1)S(1)} %joined_residual.1.refs_0_.b0, ...), custom_call_target="tpu_custom_call" | custom-call | flops 1006632960 | bytes 3145728 | tf_op jit(solution)/shard_map/project/pallas_call | solution.py:340
  40.5 1.9 %collective-permute-done.10.refs_0_.b2 = bf16[384,256]{1,0:T(8,128)(2,1)S(1)} collective-permute-done((bf16[384,256]{1,0:T(8,128)(2,1)S(1)}, bf16[384,256]{1,0:T(8,128)(2,1)S(1)}, u32[]{:S(2)}, u32[]{:S(2)}) %collective-permute-start.10) | collective-permute-done | bytes 196640 | tf_op jit(solution)/shard_map/ppermute | solution.py:458
  42.4 1.2 %project.4 = (bf16[384,1024]{1,0:T(8,128)(2,1)S(1)}, bf16[384,1024]{1,0:T(8,128)(2,1)S(1)}, bf16[192,1024]{1,0:T(8,128)(2,1)S(1)}) custom-call(s32[3]{0:T(128)S(1)} %pad_add_fusion.me, f32[4,1,256]{2,1,0:T(1,128)S(1)} %bitcast.13, bf16[1024,3072]{1,0:T(8,128)(2,1)S(1)} %bitcast.11, bf16[384,256]{1,0:T(8,128)(2,1)S(1)} %collective-permute-done.10.refs_0_.b2, ...), custom_call_target="tpu_custom_call" | custom-call | flops 503316480 | bytes 1572864 | tf_op jit(solution)/shard_map/project/pallas_call | solution.py:340
  43.6 1.5 %project.5 = (f32[384,1024]{1,0:T(8,128)S(1)}, f32[384,1024]{1,0:T(8,128)S(1)}) custom-call(s32[3]{0:T(128)S(1)} %pad_add_fusion.me, f32[4,1,256]{2,1,0:T(1,128)S(1)} %bitcast.14, bf16[1024,3072]{1,0:T(8,128)(2,1)S(1)} %bitcast.11, bf16[384,256]{1,0:T(8,128)(2,1)S(1)} %add_convert_fusion.refs_0_.b0, bf16[384,256]{1,0:T(8,128)(2,1)S(1)} %collective-permute-done.12.refs_1_.b1), custom_call_target="tpu_custom_call" | custom-call | flops 1006632960 | bytes 3145728 | tf_op jit(solution)/shard_map/project/pallas_call | solution.py:340
  45.2 0.0 copy-start
  45.2 1.6 %keys_of.1 = (bf16[384,1024]{1,0:T(8,128)(2,1)S(1)}, bf16[384,1024]{1,0:T(8,128)(2,1)S(1)}) custom-call(s32[3]{0:T(128)S(1)} %pad_add_fusion.me, bf16[384,256]{1,0:T(8,128)(2,1)S(1)} %add_convert_fusion.refs_0_.b0, bf16[384,256]{1,0:T(8,128)(2,1)S(1)} %collective-permute-done.12.refs_1_.b1, bf16[400,256]{1,0:T(8,128)(2,1)S(1)} %collective-permute-done.13.b2.bias_y, ...), custom_call_target="tpu_custom_call" | custom-call | flops 805306368 | bytes 2097152 | tf_op jit(solution)/shard_map/keys_of/pallas_call | solution.py:296
  46.8 6.5 %attend.1 = bf16[192,1024]{1,0:T(8,128)(2,1)} custom-call(s32[3]{0:T(128)S(1)} %pad_add_fusion.me, bf16[400,256]{1,0:T(8,128)(2,1)S(1)} %joined_residual.1.refs_0_.b0, bf16[400,256]{1,0:T(8,128)(2,1)S(1)} %collective-permute-done.5.refs_1_.b1, bf16[384,256]{1,0:T(8,128)(2,1)S(1)} %collective-permute-done.10.refs_0_.b2, ...), custom_call_target="tpu_custom_call" | custom-call | flops 3221225472 | bytes 8388608 | tf_op jit(solution)/shard_map/attend/pallas_call | solution.py:427
  (25 shorter events, 0.1 us)
Async XLA Ops:
  0.0 12.3 %collective-permute-start.6 = (bf16[192,1024]{1,0:T(8,128)(2,1)}, bf16[192,1024]{1,0:T(8,128)(2,1)S(1)}, u32[]{:S(2)}, u32[]{:S(2)}) collective-permute-start(bf16[192,1024]{1,0:T(8,128)(2,1)} %bitcast.17), channel_id=1, source_target_pairs={{0,8},{4,12},{8,0},{12,4},{1,9},{5,13},{9,1},{13,5},{2,10},{6,14},... | collective-permute-start | bytes 1179656 | tf_op jit(solution)/shard_map/ppermute | solution.py:458
  3.0 16.8 %collective-permute-start = (bf16[192,1024]{1,0:T(8,128)(2,1)}, bf16[192,1024]{1,0:T(8,128)(2,1)S(1)}, u32[]{:S(2)}, u32[]{:S(2)}) collective-permute-start(bf16[192,1024]{1,0:T(8,128)(2,1)} %bitcast.18), channel_id=1, source_target_pairs={{0,4},{4,0},{8,12},{12,8},{1,5},{5,1},{9,13},{13,9},{2,6},{6,2},{1... | collective-permute-start | bytes 1179656 | tf_op jit(solution)/shard_map/ppermute | solution.py:458
  12.3 11.7 %collective-permute-start.7 = (bf16[192,1024]{1,0:T(8,128)(2,1)S(1)}, bf16[192,1024]{1,0:T(8,128)(2,1)S(1)}, u32[]{:S(2)}, u32[]{:S(2)}) collective-permute-start(bf16[192,1024]{1,0:T(8,128)(2,1)S(1)} %collective-permute-done.6.xa), channel_id=1, source_target_pairs={{0,4},{4,0},{8,12},{12,8},{1,5},{5,1},{9,13},{13,9},{2,6},{6,2},{1... | collective-permute-start | bytes 1179656 | tf_op jit(solution)/shard_map/ppermute | solution.py:458
  13.1 3.9 %collective-permute-start.1 = (bf16[16,1024]{1,0:T(8,128)(2,1)S(1)}, bf16[16,1024]{1,0:T(8,128)(2,1)S(1)}, u32[]{:S(2)}, u32[]{:S(2)}) collective-permute-start(bf16[16,1024]{1,0:T(8,128)(2,1)S(1)} %dynamic-slice_bitcast_fusion), channel_id=1, source_target_pairs={{0,8},{4,12},{8,0},{12,4},{1,9},{5,13},{9,1},{13,5},{2,10},{6,14},... | collective-permute-start | bytes 98312 | tf_op jit(solution)/shard_map/ppermute | solution.py:458
  17.0 2.8 %collective-permute-start.2 = (bf16[16,1024]{1,0:T(8,128)(2,1)S(1)}, bf16[16,1024]{1,0:T(8,128)(2,1)S(1)}, u32[]{:S(2)}, u32[]{:S(2)}) collective-permute-start(bf16[16,1024]{1,0:T(8,128)(2,1)S(1)} %collective-permute-done.1.ea), channel_id=1, source_target_pairs={{0,4},{4,0},{8,12},{12,8},{1,5},{5,1},{9,13},{13,9},{2,6},{6,2},{1... | collective-permute-start | bytes 98312 | tf_op jit(solution)/shard_map/ppermute | solution.py:458
  19.8 4.2 %copy-start.2 = (bf16[1,192,16]{1,2,0:T(8,128)(2,1)S(1)}, bf16[1,192,16]{1,2,0:T(8,128)(2,1)}, u32[]{:S(2)}) copy-start(bf16[1,192,16]{1,2,0:T(8,128)(2,1)} %param.11) | copy-start | bytes 18436
  21.9 8.6 %collective-permute-start.3 = (bf16[384,256]{1,0:T(8,128)(2,1)S(1)}, bf16[384,256]{1,0:T(8,128)(2,1)S(1)}, u32[]{:S(2)}, u32[]{:S(2)}) collective-permute-start(bf16[384,256]{1,0:T(8,128)(2,1)S(1)} %get-tuple-element.32), channel_id=1, source_target_pairs={{0,1},{1,0},{2,3},{3,2},{4,5},{5,4},{6,7},{7,6},{8,9},{9,8},{10,11... | collective-permute-start | bytes 589832 | tf_op jit(solution)/shard_map/ppermute | solution.py:471
  23.7 6.8 %collective-permute-start.4 = (bf16[384,256]{1,0:T(8,128)(2,1)S(1)}, bf16[384,256]{1,0:T(8,128)(2,1)S(1)}, u32[]{:S(2)}, u32[]{:S(2)}) collective-permute-start(bf16[384,256]{1,0:T(8,128)(2,1)S(1)} %get-tuple-element.33), channel_id=1, source_target_pairs={{0,4},{1,2},{2,1},{3,7},{4,0},{5,6},{6,5},{7,3},{8,12},{9,10},{10,... | collective-permute-start | bytes 589832 | tf_op jit(solution)/shard_map/ppermute | solution.py:471
  24.0 14.7 %slice-start = ((s8[6291456]{0:T(1024)(128)(4,1)}), s8[4194304]{0:T(1024)(128)(4,1)S(1)}, s32[]{:S(2)}) async-start(s8[6291456]{0:T(1024)(128)(4,1)} %bitcast.10), calls=%async_computation | async-start | bytes 8388608
  26.1 7.5 %collective-permute-start.9 = (bf16[384,256]{1,0:T(8,128)(2,1)S(1)}, bf16[384,256]{1,0:T(8,128)(2,1)S(1)}, u32[]{:S(2)}, u32[]{:S(2)}) collective-permute-start(bf16[384,256]{1,0:T(8,128)(2,1)S(1)} %get-tuple-element.43), channel_id=1, source_target_pairs={{0,4},{1,2},{2,1},{3,7},{4,0},{5,6},{6,5},{7,3},{8,12},{9,10},{10,... | collective-permute-start | bytes 589832 | tf_op jit(solution)/shard_map/ppermute | solution.py:471
  26.4 7.8 %collective-permute-start.8 = (bf16[384,256]{1,0:T(8,128)(2,1)S(1)}, bf16[384,256]{1,0:T(8,128)(2,1)S(1)}, u32[]{:S(2)}, u32[]{:S(2)}) collective-permute-start(bf16[384,256]{1,0:T(8,128)(2,1)S(1)} %get-tuple-element.41), channel_id=1, source_target_pairs={{0,1},{1,0},{2,3},{3,2},{4,5},{5,4},{6,7},{7,6},{8,9},{9,8},{10,11... | collective-permute-start | bytes 589832 | tf_op jit(solution)/shard_map/ppermute | solution.py:471
  29.1 9.6 %slice-start.1 = ((s8[6291456]{0:T(1024)(128)(4,1)}), s8[2097152]{0:T(1024)(128)(4,1)S(1)}, s32[]{:S(2)}) async-start(s8[6291456]{0:T(1024)(128)(4,1)} %bitcast.10), calls=%async_computation.1 | async-start | bytes 4194304
  30.6 8.1 %collective-permute-start.5 = (bf16[400,256]{1,0:T(8,128)(2,1)S(1)}, bf16[400,256]{1,0:T(8,128)(2,1)S(1)}, u32[]{:S(2)}, u32[]{:S(2)}) collective-permute-start(bf16[400,256]{1,0:T(8,128)(2,1)S(1)} %joined_residual.1.refs_0_.b0), channel_id=1, source_target_pairs={{0,4},{4,0},{8,12},{12,8},{1,5},{5,1},{9,13},{13,9},{2,6},{6,2},{1... | collective-permute-start | bytes 614408 | tf_op jit(solution)/shard_map/ppermute | solution.py:458
  30.7 8.0 %collective-permute-start.13 = (bf16[400,256]{1,0:T(8,128)(2,1)S(1)}, bf16[400,256]{1,0:T(8,128)(2,1)S(1)}, u32[]{:S(2)}, u32[]{:S(2)}) collective-permute-start(bf16[400,256]{1,0:T(8,128)(2,1)S(1)} %joined_residual.1.refs_0_.b0), channel_id=1, source_target_pairs={{0,8},{4,12},{8,0},{12,4},{1,9},{5,13},{9,1},{13,5},{2,10},{6,14},... | collective-permute-start | bytes 614408 | tf_op jit(solution)/shard_map/ppermute | solution.py:458
  32.3 6.5 %copy-start.1 = (f32[1024]{0:T(1024)S(1)}, f32[1024]{0:T(1024)}, u32[]{:S(2)}) copy-start(f32[1024]{0:T(1024)} %param.8) | copy-start | bytes 12292
  34.3 8.1 %collective-permute-start.10 = (bf16[384,256]{1,0:T(8,128)(2,1)S(1)}, bf16[384,256]{1,0:T(8,128)(2,1)S(1)}, u32[]{:S(2)}, u32[]{:S(2)}) collective-permute-start(bf16[384,256]{1,0:T(8,128)(2,1)S(1)} %add_convert_fusion.refs_0_.b0), channel_id=1, source_target_pairs={{0,8},{4,12},{8,0},{12,4},{1,9},{5,13},{9,1},{13,5},{2,10},{6,14},... | collective-permute-start | bytes 589832 | tf_op jit(solution)/shard_map/ppermute | solution.py:458
  35.9 7.7 %collective-permute-start.12 = (bf16[384,256]{1,0:T(8,128)(2,1)S(1)}, bf16[384,256]{1,0:T(8,128)(2,1)S(1)}, u32[]{:S(2)}, u32[]{:S(2)}) collective-permute-start(bf16[384,256]{1,0:T(8,128)(2,1)S(1)} %add_convert_fusion.refs_0_.b0), channel_id=1, source_target_pairs={{0,4},{4,0},{8,12},{12,8},{1,5},{5,1},{9,13},{13,9},{2,6},{6,2},{1... | collective-permute-start | bytes 589832 | tf_op jit(solution)/shard_map/ppermute | solution.py:458
  38.7 6.5 %collective-permute-start.14 = (bf16[400,256]{1,0:T(8,128)(2,1)S(1)}, bf16[400,256]{1,0:T(8,128)(2,1)S(1)}, u32[]{:S(2)}, u32[]{:S(2)}) collective-permute-start(bf16[400,256]{1,0:T(8,128)(2,1)S(1)} %collective-permute-done.13.b2.bias_y), channel_id=1, source_target_pairs={{0,4},{4,0},{8,12},{12,8},{1,5},{5,1},{9,13},{13,9},{2,6},{6,2},{1... | collective-permute-start | bytes 614408 | tf_op jit(solution)/shard_map/ppermute | solution.py:458
  42.4 4.4 %collective-permute-start.11 = (bf16[384,256]{1,0:T(8,128)(2,1)S(1)}, bf16[384,256]{1,0:T(8,128)(2,1)S(1)}, u32[]{:S(2)}, u32[]{:S(2)}) collective-permute-start(bf16[384,256]{1,0:T(8,128)(2,1)S(1)} %collective-permute-done.10.refs_0_.b2), channel_id=1, source_target_pairs={{0,4},{4,0},{8,12},{12,8},{1,5},{5,1},{9,13},{13,9},{2,6},{6,2},{1... | collective-permute-start | bytes 589832 | tf_op jit(solution)/shard_map/ppermute | solution.py:458
  45.2 1.6 %copy-start = (bf16[1024,1024]{1,0:T(8,128)(2,1)S(1)}, bf16[1024,1024]{1,0:T(8,128)(2,1)}, u32[]{:S(2)}) copy-start(bf16[1024,1024]{1,0:T(8,128)(2,1)} %w_out.1) | copy-start | bytes 6291460

commit v4 on v3

--- a/solution.py
+++ b/solution.py
@@ -280,7 +280,7 @@
     parts = [scaled(blocks[k], gain, lane, k, rows) for k in steps]
     factor = factor_of(blocks, 0, rows, ch)
     for out, acc, first in ((k_out, key_sum, ch), (v_out, value_sum, 2 * ch)):
-        total = acc[...]
+        total = acc[...].astype(F32)
         for k, part in zip(steps, parts):
             at = pl.multiple_of((lane ^ k) * width, width)
             total = total + jnp.dot(
@@ -326,7 +326,7 @@
     ]
     for i, out in enumerate(outs):
         first, use = ((ch, parts), (2 * ch, parts), (0, owns))[i]
-        acc = olds[i][...] if olds else None
+        acc = olds[i][...].astype(F32) if olds else None
         for k, part in zip(steps, use):
             at = pl.multiple_of((lane ^ k) * width, width)
             term = jnp.dot(part, w[pl.ds(at, width), first : first + ch], preferred_element_type=F32)
@@ -501,11 +501,11 @@
     near_d = swap(near_y, 1)
 
     gain = norm_gain.reshape(lon_size, 1, width)
-    far_sums = project(me, (0, 1), (far, far_c), gain, qkv_weight, n, count=2)
+    far_sums = project(me, (0, 1), (far, far_c), gain, qkv_weight, n, count=2, dtype=BF16)
     k_far, v_far = keys_of(
         me, (2, 3), (far, far_c, far_y, far_d), gain, qkv_weight, far_sums
     )
-    sums = project(me, (0, 1), (near, near_c), gain, qkv_weight, n)
+    sums = project(me, (0, 1), (near, near_c), gain, qkv_weight, n, dtype=BF16)
     sums = project(me, (2,), (near_y,), gain, qkv_weight, n, sums, dtype=BF16)
     out = attend(
         me, (3,), (near, near_c, near_y, near_d), gain, qkv_weight, sums, k_far, v_far, far_y,

time: 53.7 us -> 53.8 us (level)
  transfers between devices with their start and end apart: 15 -> 15, of which waited for: 5 -> 5; matrix products, arithmetic and copies ran while one was open for 2% -> 2% of each run, Pallas kernels for 29% -> 30%
where the time goes in v4:
time: 53.8 us; the launch traced here: 53.4 us
  Pallas kernels  22.2 us (41%)
  waiting for transfers between devices  16.8 us (31%)
  starting transfers between devices  13.2 us (25%)
  local copies, waits for them, and re-layouts  0.79 us (1%)
    ppermute x11, waiting for transfers between devices, swap(): return lax.ppermute(value, 'lon', [(i, i ^ bit) for i in range(lon_size)])  16.2 us
    ppermute x11, starting transfers between devices, swap(): return lax.ppermute(value, 'lon', [(i, i ^ bit) for i in range(lon_size)])  7.99 us
    pallas_call x1, Pallas kernels, attend(): pl.pallas_call(functools.partial(attend_kernel, steps), out_shape=jax.Sha...  6.41 us
    ppermute x4, starting transfers between devices, lat_swap(): return lax.ppermute(value, ('lon', 'lat'), pairs)  5.16 us
    pallas_call x3, Pallas kernels, project(): pl.pallas_call(functools.partial(project_kernel, steps, count), out_shape...  4.64 us
    pallas_call x2, Pallas kernels, conv_sides(): pl.pallas_call(conv_kernel, out_shape=(vout((2 * n, width), BF16), vout((...  4.15 us
    pallas_call x1, Pallas kernels, load(): pl.pallas_call(functools.partial(load_kernel, tuple(pieces)), out_shape=t...  2.66 us
    pallas_call x2, Pallas kernels, conv_middle(): pl.pallas_call(middle_kernel, out_shape=(vout((rows, width), F32), vout((...  2.62 us
  transfers between devices with their start and end apart: 15, of which 5 were waited for; matrix products, arithmetic and copies ran while one was open for 2% of the time, Pallas kernels for 30%

profile of v4, /device:TPU:0, one launch (start us, length us, event | category | flops | bytes accessed | tf_op | source)
XLA Modules:
  0.0 53.4 jit_solution(86677584019163898)
XLA Ops:
  0.0 3.0 %collective-permute-start.6 = (bf16[192,1024]{1,0:T(8,128)(2,1)}, bf16[192,1024]{1,0:T(8,128)(2,1)S(1)}, u32[]{:S(2)}, u32[]{:S(2)}) collective-permute-start(bf16[192,1024]{1,0:T(8,128)(2,1)} %bitcast.17), channel_id=1, source_target_pairs={{0,8},{4,12},{8,0},{12,4},{1,9},{5,13},{9,1},{13,5},{2,10},{6,14},... | collective-permute-start | bytes 1179656 | tf_op jit(solution)/shard_map/ppermute | solution.py:458
  3.0 0.0 collective-permute-start
  3.0 9.3 %collective-permute-done.6.xa = bf16[192,1024]{1,0:T(8,128)(2,1)S(1)} collective-permute-done((bf16[192,1024]{1,0:T(8,128)(2,1)}, bf16[192,1024]{1,0:T(8,128)(2,1)S(1)}, u32[]{:S(2)}, u32[]{:S(2)}) %collective-permute-start.6) | collective-permute-done | bytes 393248 | tf_op jit(solution)/shard_map/ppermute | solution.py:458
  12.3 0.8 %dynamic-slice_bitcast_fusion = bf16[16,1024]{1,0:T(8,128)(2,1)S(1)} fusion(bf16[1,192,1024]{2,1,0:T(8,128)(2,1)} %param.6, s32[]{:T(128)S(6)} %select_n.15), kind=kLoop, calls=%fused_computation.2 | loop fusion | bytes 65540 | tf_op jit(solution)/shard_map/dynamic_slice | solution.py:474
  13.1 1.7 %collective-permute-start.1 = (bf16[16,1024]{1,0:T(8,128)(2,1)S(1)}, bf16[16,1024]{1,0:T(8,128)(2,1)S(1)}, u32[]{:S(2)}, u32[]{:S(2)}) collective-permute-start(bf16[16,1024]{1,0:T(8,128)(2,1)S(1)} %dynamic-slice_bitcast_fusion), channel_id=1, source_target_pairs={{0,8},{4,12},{8,0},{12,4},{1,9},{5,13},{9,1},{13,5},{2,10},{6,14},... | collective-permute-start | bytes 98312 | tf_op jit(solution)/shard_map/ppermute | solution.py:458
  14.8 2.2 %collective-permute-done.1.ea = bf16[16,1024]{1,0:T(8,128)(2,1)S(1)} collective-permute-done((bf16[16,1024]{1,0:T(8,128)(2,1)S(1)}, bf16[16,1024]{1,0:T(8,128)(2,1)S(1)}, u32[]{:S(2)}, u32[]{:S(2)}) %collective-permute-start.1) | collective-permute-done | bytes 32800 | tf_op jit(solution)/shard_map/ppermute | solution.py:458
  17.0 0.1 pad_add_fusion.me
  17.1 2.7 %load.1 = (bf16[192,1024]{1,0:T(8,128)(2,1)S(1)}, bf16[6144,256]{1,0:T(8,128)(2,1)S(1)}, bf16[3072,256]{1,0:T(8,128)(2,1)S(1)}) custom-call(bf16[192,1024]{1,0:T(8,128)(2,1)} %bitcast.19, bf16[9216,256]{1,0:T(8,128)(2,1)} %refs_2_.1, bf16[9216,256]{1,0:T(8,128)(2,1)} %refs_2_.1), custom_call_target="tpu_custom_call" | custom-call | bytes 5111808 | tf_op jit(solution)/shard_map/load/pallas_call | solution.py:152
  19.7 0.0 copy-start.2
  19.8 2.1 %conv_sides.2 = (bf16[384,256]{1,0:T(8,128)(2,1)S(1)}, bf16[384,256]{1,0:T(8,128)(2,1)S(1)}, bf16[384,3072]{1,0:T(8,128)(2,1)S(1)}) custom-call(s32[3]{0:T(128)S(1)} %pad_add_fusion.me, bf16[192,1024]{1,0:T(8,128)(2,1)S(1)} %get-tuple-element.30.xa.ea, bf16[192,1024]{1,0:T(8,128)(2,1)S(1)} %collective-permute-done.xb.eb, ...), custom_call_target="tpu_custom_call" | custom-call | flops 1207959552 | bytes 3145728 | tf_op jit(solution)/shard_map/conv_sides/pallas_call | solution.py:190
  21.9 1.9 %collective-permute-start.3 = (bf16[384,256]{1,0:T(8,128)(2,1)S(1)}, bf16[384,256]{1,0:T(8,128)(2,1)S(1)}, u32[]{:S(2)}, u32[]{:S(2)}) collective-permute-start(bf16[384,256]{1,0:T(8,128)(2,1)S(1)} %get-tuple-element.32), channel_id=1, source_target_pairs={{0,1},{1,0},{2,3},{3,2},{4,5},{5,4},{6,7},{7,6},{8,9},{9,8},{10,11... | collective-permute-start | bytes 589832 | tf_op jit(solution)/shard_map/ppermute | solution.py:471
  23.7 0.3 collective-permute-start.4
  24.0 0.0 slice-start
  24.0 2.1 %conv_sides.3 = (bf16[384,256]{1,0:T(8,128)(2,1)S(1)}, bf16[384,256]{1,0:T(8,128)(2,1)S(1)}, bf16[384,3072]{1,0:T(8,128)(2,1)S(1)}) custom-call(s32[3]{0:T(128)S(1)} %pad_add_fusion.me, bf16[192,1024]{1,0:T(8,128)(2,1)S(1)} %collective-permute-done.6.xa, bf16[192,1024]{1,0:T(8,128)(2,1)S(1)} %collective-permute-done.7.xb, ...), custom_call_target="tpu_custom_call" | custom-call | flops 1207959552 | bytes 3145728 | tf_op jit(solution)/shard_map/conv_sides/pallas_call | solution.py:190
  26.1 0.3 collective-permute-start.9
  26.4 2.7 %collective-permute-start.8 = (bf16[384,256]{1,0:T(8,128)(2,1)S(1)}, bf16[384,256]{1,0:T(8,128)(2,1)S(1)}, u32[]{:S(2)}, u32[]{:S(2)}) collective-permute-start(bf16[384,256]{1,0:T(8,128)(2,1)S(1)} %get-tuple-element.41), channel_id=1, source_target_pairs={{0,1},{1,0},{2,3},{3,2},{4,5},{5,4},{6,7},{7,6},{8,9},{9,8},{10,11... | collective-permute-start | bytes 589832 | tf_op jit(solution)/shard_map/ppermute | solution.py:471
  29.1 1.3 %conv_middle.2 = (f32[384,256]{1,0:T(8,128)S(1)}, f32[384,256]{1,0:T(8,128)S(1)}, f32[1,256]{1,0:T(1,128)S(1)}) custom-call(s32[3]{0:T(128)S(1)} %pad_add_fusion.me, bf16[384,3072]{1,0:T(8,128)(2,1)S(1)} %get-tuple-element.34.cols, bf16[3072,256]{1,0:T(8,128)(2,1)S(1)} %get-tuple-element.35.w), custom_call_target="tpu_custom_call" | custom-call | flops 603979776 | bytes 1572864 | tf_op jit(solution)/shard_map/conv_middle/pallas_call | solution.py:221
  30.5 0.1 joined_residual.1.refs_0_.b0
  30.6 0.1 collective-permute-start.5
  30.7 1.6 %collective-permute-start.13 = (bf16[400,256]{1,0:T(8,128)(2,1)S(1)}, bf16[400,256]{1,0:T(8,128)(2,1)S(1)}, u32[]{:S(2)}, u32[]{:S(2)}) collective-permute-start(bf16[400,256]{1,0:T(8,128)(2,1)S(1)} %joined_residual.1.refs_0_.b0), channel_id=1, source_target_pairs={{0,8},{4,12},{8,0},{12,4},{1,9},{5,13},{9,1},{13,5},{2,10},{6,14},... | collective-permute-start | bytes 614408 | tf_op jit(solution)/shard_map/ppermute | solution.py:458
  32.3 1.3 %conv_middle.3 = (f32[384,256]{1,0:T(8,128)S(1)}, f32[384,256]{1,0:T(8,128)S(1)}, f32[1,256]{1,0:T(1,128)S(1)}) custom-call(s32[3]{0:T(128)S(1)} %pad_add_fusion.me, bf16[384,3072]{1,0:T(8,128)(2,1)S(1)} %get-tuple-element.39.cols, bf16[3072,256]{1,0:T(8,128)(2,1)S(1)} %get-tuple-element.35.w), custom_call_target="tpu_custom_call" | custom-call | flops 603979776 | bytes 1572864 | tf_op jit(solution)/shard_map/conv_middle/pallas_call | solution.py:221
  33.6 0.6 %collective-permute-done.8 = bf16[384,256]{1,0:T(8,128)(2,1)S(1)} collective-permute-done((bf16[384,256]{1,0:T(8,128)(2,1)S(1)}, bf16[384,256]{1,0:T(8,128)(2,1)S(1)}, u32[]{:S(2)}, u32[]{:S(2)}) %collective-permute-start.8) | collective-permute-done | bytes 196640 | tf_op jit(solution)/shard_map/ppermute | solution.py:471
  34.2 0.1 add_convert_fusion.refs_0_.b0
  34.3 1.6 %collective-permute-start.10 = (bf16[384,256]{1,0:T(8,128)(2,1)S(1)}, bf16[384,256]{1,0:T(8,128)(2,1)S(1)}, u32[]{:S(2)}, u32[]{:S(2)}) collective-permute-start(bf16[384,256]{1,0:T(8,128)(2,1)S(1)} %add_convert_fusion.refs_0_.b0), channel_id=1, source_target_pairs={{0,8},{4,12},{8,0},{12,4},{1,9},{5,13},{9,1},{13,5},{2,10},{6,14},... | collective-permute-start | bytes 589832 | tf_op jit(solution)/shard_map/ppermute | solution.py:458
  35.9 2.8 %collective-permute-done.13.b2.bias_y = bf16[400,256]{1,0:T(8,128)(2,1)S(1)} collective-permute-done((bf16[400,256]{1,0:T(8,128)(2,1)S(1)}, bf16[400,256]{1,0:T(8,128)(2,1)S(1)}, u32[]{:S(2)}, u32[]{:S(2)}) %collective-permute-start.13) | collective-permute-done | bytes 204832 | tf_op jit(solution)/shard_map/ppermute | solution.py:458
  38.7 1.7 %project.3 = (bf16[384,1024]{1,0:T(8,128)(2,1)S(1)}, bf16[384,1024]{1,0:T(8,128)(2,1)S(1)}, bf16[192,1024]{1,0:T(8,128)(2,1)S(1)}) custom-call(s32[3]{0:T(128)S(1)} %pad_add_fusion.me, f32[4,1,256]{2,1,0:T(1,128)S(1)} %bitcast.12, bf16[1024,3072]{1,0:T(8,128)(2,1)S(1)} %bitcast.11, bf16[400,256]{1,0:T(8,128)(2,1)S(1)} %joined_residual.1.refs_0_.b0, ...), custom_call_target="tpu_custom_call" | custom-call | flops 1006632960 | bytes 3145728 | tf_op jit(solution)/shard_map/project/pallas_call | solution.py:340
  40.5 1.9 %collective-permute-done.10.refs_0_.b2 = bf16[384,256]{1,0:T(8,128)(2,1)S(1)} collective-permute-done((bf16[384,256]{1,0:T(8,128)(2,1)S(1)}, bf16[384,256]{1,0:T(8,128)(2,1)S(1)}, u32[]{:S(2)}, u32[]{:S(2)}) %collective-permute-start.10) | collective-permute-done | bytes 196640 | tf_op jit(solution)/shard_map/ppermute | solution.py:458
  42.4 1.4 %project.4 = (bf16[384,1024]{1,0:T(8,128)(2,1)S(1)}, bf16[384,1024]{1,0:T(8,128)(2,1)S(1)}, bf16[192,1024]{1,0:T(8,128)(2,1)S(1)}) custom-call(s32[3]{0:T(128)S(1)} %pad_add_fusion.me, f32[4,1,256]{2,1,0:T(1,128)S(1)} %bitcast.13, bf16[1024,3072]{1,0:T(8,128)(2,1)S(1)} %bitcast.11, ...), custom_call_target="tpu_custom_call", output_to_operand_aliasing={{0}: (4, {}), {1}: (5, {}), {2}: (6, {})} | custom-call | flops 503316480 | bytes 1572864 | tf_op jit(solution)/shard_map/project/pallas_call | solution.py:340
  43.8 1.5 %project.5 = (bf16[384,1024]{1,0:T(8,128)(2,1)S(1)}, bf16[384,1024]{1,0:T(8,128)(2,1)S(1)}) custom-call(s32[3]{0:T(128)S(1)} %pad_add_fusion.me, f32[4,1,256]{2,1,0:T(1,128)S(1)} %bitcast.14, bf16[1024,3072]{1,0:T(8,128)(2,1)S(1)} %bitcast.11, bf16[384,256]{1,0:T(8,128)(2,1)S(1)} %add_convert_fusion.refs_0_.b0, ...), custom_call_target="tpu_custom_call" | custom-call | flops 1006632960 | bytes 3145728 | tf_op jit(solution)/shard_map/project/pallas_call | solution.py:340
  45.3 0.0 copy-start
  45.3 1.6 %keys_of.1 = (bf16[384,1024]{1,0:T(8,128)(2,1)S(1)}, bf16[384,1024]{1,0:T(8,128)(2,1)S(1)}) custom-call(s32[3]{0:T(128)S(1)} %pad_add_fusion.me, bf16[384,256]{1,0:T(8,128)(2,1)S(1)} %add_convert_fusion.refs_0_.b0, bf16[384,256]{1,0:T(8,128)(2,1)S(1)} %collective-permute-done.12.refs_1_.b1, bf16[400,256]{1,0:T(8,128)(2,1)S(1)} %collective-permute-done.13.b2.bias_y, ...), custom_call_target="tpu_custom_call" | custom-call | flops 805306368 | bytes 2097152 | tf_op jit(solution)/shard_map/keys_of/pallas_call | solution.py:296
  47.0 6.4 %attend.1 = bf16[192,1024]{1,0:T(8,128)(2,1)} custom-call(s32[3]{0:T(128)S(1)} %pad_add_fusion.me, bf16[400,256]{1,0:T(8,128)(2,1)S(1)} %joined_residual.1.refs_0_.b0, bf16[400,256]{1,0:T(8,128)(2,1)S(1)} %collective-permute-done.5.refs_1_.b1, bf16[384,256]{1,0:T(8,128)(2,1)S(1)} %collective-permute-done.10.refs_0_.b2, ...), custom_call_target="tpu_custom_call" | custom-call | flops 3221225472 | bytes 8388608 | tf_op jit(solution)/shard_map/attend/pallas_call | solution.py:427
  (25 shorter events, 0.1 us)
Async XLA Ops:
  0.0 12.3 %collective-permute-start.6 = (bf16[192,1024]{1,0:T(8,128)(2,1)}, bf16[192,1024]{1,0:T(8,128)(2,1)S(1)}, u32[]{:S(2)}, u32[]{:S(2)}) collective-permute-start(bf16[192,1024]{1,0:T(8,128)(2,1)} %bitcast.17), channel_id=1, source_target_pairs={{0,8},{4,12},{8,0},{12,4},{1,9},{5,13},{9,1},{13,5},{2,10},{6,14},... | collective-permute-start | bytes 1179656 | tf_op jit(solution)/shard_map/ppermute | solution.py:458
  3.0 16.8 %collective-permute-start = (bf16[192,1024]{1,0:T(8,128)(2,1)}, bf16[192,1024]{1,0:T(8,128)(2,1)S(1)}, u32[]{:S(2)}, u32[]{:S(2)}) collective-permute-start(bf16[192,1024]{1,0:T(8,128)(2,1)} %bitcast.18), channel_id=1, source_target_pairs={{0,4},{4,0},{8,12},{12,8},{1,5},{5,1},{9,13},{13,9},{2,6},{6,2},{1... | collective-permute-start | bytes 1179656 | tf_op jit(solution)/shard_map/ppermute | solution.py:458
  12.3 11.7 %collective-permute-start.7 = (bf16[192,1024]{1,0:T(8,128)(2,1)S(1)}, bf16[192,1024]{1,0:T(8,128)(2,1)S(1)}, u32[]{:S(2)}, u32[]{:S(2)}) collective-permute-start(bf16[192,1024]{1,0:T(8,128)(2,1)S(1)} %collective-permute-done.6.xa), channel_id=1, source_target_pairs={{0,4},{4,0},{8,12},{12,8},{1,5},{5,1},{9,13},{13,9},{2,6},{6,2},{1... | collective-permute-start | bytes 1179656 | tf_op jit(solution)/shard_map/ppermute | solution.py:458
  13.1 3.9 %collective-permute-start.1 = (bf16[16,1024]{1,0:T(8,128)(2,1)S(1)}, bf16[16,1024]{1,0:T(8,128)(2,1)S(1)}, u32[]{:S(2)}, u32[]{:S(2)}) collective-permute-start(bf16[16,1024]{1,0:T(8,128)(2,1)S(1)} %dynamic-slice_bitcast_fusion), channel_id=1, source_target_pairs={{0,8},{4,12},{8,0},{12,4},{1,9},{5,13},{9,1},{13,5},{2,10},{6,14},... | collective-permute-start | bytes 98312 | tf_op jit(solution)/shard_map/ppermute | solution.py:458
  17.0 2.8 %collective-permute-start.2 = (bf16[16,1024]{1,0:T(8,128)(2,1)S(1)}, bf16[16,1024]{1,0:T(8,128)(2,1)S(1)}, u32[]{:S(2)}, u32[]{:S(2)}) collective-permute-start(bf16[16,1024]{1,0:T(8,128)(2,1)S(1)} %collective-permute-done.1.ea), channel_id=1, source_target_pairs={{0,4},{4,0},{8,12},{12,8},{1,5},{5,1},{9,13},{13,9},{2,6},{6,2},{1... | collective-permute-start | bytes 98312 | tf_op jit(solution)/shard_map/ppermute | solution.py:458
  19.7 4.2 %copy-start.2 = (bf16[1,192,16]{1,2,0:T(8,128)(2,1)S(1)}, bf16[1,192,16]{1,2,0:T(8,128)(2,1)}, u32[]{:S(2)}) copy-start(bf16[1,192,16]{1,2,0:T(8,128)(2,1)} %param.11) | copy-start | bytes 18436
  21.9 8.6 %collective-permute-start.3 = (bf16[384,256]{1,0:T(8,128)(2,1)S(1)}, bf16[384,256]{1,0:T(8,128)(2,1)S(1)}, u32[]{:S(2)}, u32[]{:S(2)}) collective-permute-start(bf16[384,256]{1,0:T(8,128)(2,1)S(1)} %get-tuple-element.32), channel_id=1, source_target_pairs={{0,1},{1,0},{2,3},{3,2},{4,5},{5,4},{6,7},{7,6},{8,9},{9,8},{10,11... | collective-permute-start | bytes 589832 | tf_op jit(solution)/shard_map/ppermute | solution.py:471
  23.7 6.8 %collective-permute-start.4 = (bf16[384,256]{1,0:T(8,128)(2,1)S(1)}, bf16[384,256]{1,0:T(8,128)(2,1)S(1)}, u32[]{:S(2)}, u32[]{:S(2)}) collective-permute-start(bf16[384,256]{1,0:T(8,128)(2,1)S(1)} %get-tuple-element.33), channel_id=1, source_target_pairs={{0,4},{1,2},{2,1},{3,7},{4,0},{5,6},{6,5},{7,3},{8,12},{9,10},{10,... | collective-permute-start | bytes 589832 | tf_op jit(solution)/shard_map/ppermute | solution.py:471
  24.0 14.7 %slice-start = ((s8[6291456]{0:T(1024)(128)(4,1)}), s8[4194304]{0:T(1024)(128)(4,1)S(1)}, s32[]{:S(2)}) async-start(s8[6291456]{0:T(1024)(128)(4,1)} %bitcast.10), calls=%async_computation | async-start | bytes 8388608
  26.1 7.5 %collective-permute-start.9 = (bf16[384,256]{1,0:T(8,128)(2,1)S(1)}, bf16[384,256]{1,0:T(8,128)(2,1)S(1)}, u32[]{:S(2)}, u32[]{:S(2)}) collective-permute-start(bf16[384,256]{1,0:T(8,128)(2,1)S(1)} %get-tuple-element.43), channel_id=1, source_target_pairs={{0,4},{1,2},{2,1},{3,7},{4,0},{5,6},{6,5},{7,3},{8,12},{9,10},{10,... | collective-permute-start | bytes 589832 | tf_op jit(solution)/shard_map/ppermute | solution.py:471
  26.4 7.8 %collective-permute-start.8 = (bf16[384,256]{1,0:T(8,128)(2,1)S(1)}, bf16[384,256]{1,0:T(8,128)(2,1)S(1)}, u32[]{:S(2)}, u32[]{:S(2)}) collective-permute-start(bf16[384,256]{1,0:T(8,128)(2,1)S(1)} %get-tuple-element.41), channel_id=1, source_target_pairs={{0,1},{1,0},{2,3},{3,2},{4,5},{5,4},{6,7},{7,6},{8,9},{9,8},{10,11... | collective-permute-start | bytes 589832 | tf_op jit(solution)/shard_map/ppermute | solution.py:471
  29.1 9.6 %slice-start.1 = ((s8[6291456]{0:T(1024)(128)(4,1)}), s8[2097152]{0:T(1024)(128)(4,1)S(1)}, s32[]{:S(2)}) async-start(s8[6291456]{0:T(1024)(128)(4,1)} %bitcast.10), calls=%async_computation.1 | async-start | bytes 4194304
  30.6 8.1 %collective-permute-start.5 = (bf16[400,256]{1,0:T(8,128)(2,1)S(1)}, bf16[400,256]{1,0:T(8,128)(2,1)S(1)}, u32[]{:S(2)}, u32[]{:S(2)}) collective-permute-start(bf16[400,256]{1,0:T(8,128)(2,1)S(1)} %joined_residual.1.refs_0_.b0), channel_id=1, source_target_pairs={{0,4},{4,0},{8,12},{12,8},{1,5},{5,1},{9,13},{13,9},{2,6},{6,2},{1... | collective-permute-start | bytes 614408 | tf_op jit(solution)/shard_map/ppermute | solution.py:458
  30.7 8.0 %collective-permute-start.13 = (bf16[400,256]{1,0:T(8,128)(2,1)S(1)}, bf16[400,256]{1,0:T(8,128)(2,1)S(1)}, u32[]{:S(2)}, u32[]{:S(2)}) collective-permute-start(bf16[400,256]{1,0:T(8,128)(2,1)S(1)} %joined_residual.1.refs_0_.b0), channel_id=1, source_target_pairs={{0,8},{4,12},{8,0},{12,4},{1,9},{5,13},{9,1},{13,5},{2,10},{6,14},... | collective-permute-start | bytes 614408 | tf_op jit(solution)/shard_map/ppermute | solution.py:458
  32.3 6.5 %copy-start.1 = (f32[1024]{0:T(1024)S(1)}, f32[1024]{0:T(1024)}, u32[]{:S(2)}) copy-start(f32[1024]{0:T(1024)} %param.8) | copy-start | bytes 12292
  34.3 8.1 %collective-permute-start.10 = (bf16[384,256]{1,0:T(8,128)(2,1)S(1)}, bf16[384,256]{1,0:T(8,128)(2,1)S(1)}, u32[]{:S(2)}, u32[]{:S(2)}) collective-permute-start(bf16[384,256]{1,0:T(8,128)(2,1)S(1)} %add_convert_fusion.refs_0_.b0), channel_id=1, source_target_pairs={{0,8},{4,12},{8,0},{12,4},{1,9},{5,13},{9,1},{13,5},{2,10},{6,14},... | collective-permute-start | bytes 589832 | tf_op jit(solution)/shard_map/ppermute | solution.py:458
  35.9 7.9 %collective-permute-start.12 = (bf16[384,256]{1,0:T(8,128)(2,1)S(1)}, bf16[384,256]{1,0:T(8,128)(2,1)S(1)}, u32[]{:S(2)}, u32[]{:S(2)}) collective-permute-start(bf16[384,256]{1,0:T(8,128)(2,1)S(1)} %add_convert_fusion.refs_0_.b0), channel_id=1, source_target_pairs={{0,4},{4,0},{8,12},{12,8},{1,5},{5,1},{9,13},{13,9},{2,6},{6,2},{1... | collective-permute-start | bytes 589832 | tf_op jit(solution)/shard_map/ppermute | solution.py:458
  38.7 6.6 %collective-permute-start.14 = (bf16[400,256]{1,0:T(8,128)(2,1)S(1)}, bf16[400,256]{1,0:T(8,128)(2,1)S(1)}, u32[]{:S(2)}, u32[]{:S(2)}) collective-permute-start(bf16[400,256]{1,0:T(8,128)(2,1)S(1)} %collective-permute-done.13.b2.bias_y), channel_id=1, source_target_pairs={{0,4},{4,0},{8,12},{12,8},{1,5},{5,1},{9,13},{13,9},{2,6},{6,2},{1... | collective-permute-start | bytes 614408 | tf_op jit(solution)/shard_map/ppermute | solution.py:458
  42.4 4.6 %collective-permute-start.11 = (bf16[384,256]{1,0:T(8,128)(2,1)S(1)}, bf16[384,256]{1,0:T(8,128)(2,1)S(1)}, u32[]{:S(2)}, u32[]{:S(2)}) collective-permute-start(bf16[384,256]{1,0:T(8,128)(2,1)S(1)} %collective-permute-done.10.refs_0_.b2), channel_id=1, source_target_pairs={{0,4},{4,0},{8,12},{12,8},{1,5},{5,1},{9,13},{13,9},{2,6},{6,2},{1... | collective-permute-start | bytes 589832 | tf_op jit(solution)/shard_map/ppermute | solution.py:458
  45.3 1.6 %copy-start = (bf16[1024,1024]{1,0:T(8,128)(2,1)S(1)}, bf16[1024,1024]{1,0:T(8,128)(2,1)}, u32[]{:S(2)}) copy-start(bf16[1024,1024]{1,0:T(8,128)(2,1)} %w_out.1) | copy-start | bytes 6291460
